TPU v7x, 512 devices: a whole 4x8x8 slice. The times are simulated.
512 devices in a mesh: band: 64 (over x, y, z_hi), pw: 8 (over z_lo, core).
Axes of the slice: x: 4, y: 8, z: 8 (z_hi: 2, z_lo: 4; z = z_hi * 4 + z_lo), core: 2. Of those that a mesh axis runs over, the one named last changes fastest.
Arguments:
- occupied: bfloat16 [2, 64, 4096], P(None, 'pw'), may hold values from -6 to 6
- virtual: bfloat16 [64, 64, 4096], P('band', 'pw'), may hold values from -6 to 6
- screening: bfloat16 [16384, 16384], P('pw', 'band'), may hold values from -0.046875 to 0.046875
- grid_index: int32 [16384], replicated, may hold values from 0 to 262143, as said below
Outputs:
- grad_vir: float32 [64, 64, 4096], P('band', 'pw')
Inputs may be any that keep to these rules, and one draw needn't show every extreme that they name: `grid_index`: all entries are distinct. Write each entry as (kx * 64 + ky) * 64 + kz and take kx, ky, kz as signed frequencies (a value k of 32 or more stands for k - 64): every signed frequency lies within -16 to 16, and some entry has |kx| = |ky| = |kz| = 16. The entries g with g // 2048 = b are grid points whose ky is congruent to b modulo 64 // 8.
All inputs are finite; a program needn't handle non-finite values.
Results may differ from a plain program's by a relative error of at most 0.006.
Values may be sent and summed in bfloat16 or wider, within the bound.
A program may use at most 128 MiB of HBM per device.

v0:
```python
import math

import jax
import jax.numpy as jnp
from jax import lax
from jax.sharding import PartitionSpec as P

GRID = 64
NG = 16384


PRECISE = lax.Precision.HIGHEST


def grouped_exchange(array, axis, split_dim, concat_dim, work, item_dim, out_dim):
    items = jax.tree.leaves(array)[0].shape[item_dim]
    count = 2 if items % 2 == 0 else 1
    finished = []
    for k in range(count):
        group = jax.tree.map(
            lambda a: lax.slice_in_dim(
                a, k * (items // count), (k + 1) * (items // count), axis=item_dim
            ),
            array,
        )
        finished.append(
            work(
                lax.all_to_all(
                    group, axis, split_axis=split_dim, concat_axis=concat_dim, tiled=True
                )
            )
        )
    return jax.tree.map(lambda *parts: jnp.concatenate(parts, axis=out_dim), *finished)


def from_everyone(array, axis):
    devices = lax.axis_size(axis)
    return lax.all_to_all(
        jnp.broadcast_to(array[None], (devices, *array.shape)), axis, 0, 0, tiled=True
    )


def joined_along(tiles, dim):
    tiles = jnp.moveaxis(tiles, 0, dim)
    dims = tiles.shape
    return tiles.reshape(*dims[:dim], dims[dim] * dims[dim + 1], *dims[dim + 2 :])


def gathered_copies(array, axis, dim):
    tiles = from_everyone(array, axis)
    return joined_along(tiles, dim)


def in_blocks(array, dim, devices):
    before, after = (array.shape[:dim], array.shape[dim + 1 :])
    return jnp.moveaxis(array.reshape(*before, devices, -1, *after), dim, 0)


def sent_and_summed(array, axis, dim):
    devices = lax.axis_size(axis)
    tiles = lax.all_to_all(in_blocks(array, dim, devices), axis, 0, 0, tiled=True)
    return jnp.sum(tiles, axis=0)


def phase_pair(left_ids, right_indices, count):
    turns = left_ids[:, None] * right_indices[None, :] % count
    angles = turns.astype(jnp.float32) * (2.0 * math.pi / count)
    return (jnp.cos(angles), jnp.sin(angles))


def transform(field, cosine_table, sine_table, direction, spec):
    half_width = field.shape[-1] // 2
    times_cosine = jnp.einsum(spec, field, cosine_table, precision=PRECISE)
    with_sin = jnp.einsum(spec, field, sine_table, precision=PRECISE)
    real_part = times_cosine[..., :half_width] - direction * with_sin[..., half_width:]
    imag_part = times_cosine[..., half_width:] + direction * with_sin[..., :half_width]
    return jnp.concatenate([real_part, imag_part], axis=-1)


def body(occupied, virtual, screening, grid_index):
    occupied_count = occupied.shape[0]
    vir_count = virtual.shape[0]
    plane_count = virtual.shape[1]
    pw_count = lax.axis_size("pw")
    band_count = lax.axis_size("band")
    rows_slab = GRID // pw_count
    pair_count = occupied_count * vir_count
    slab_pos = lax.axis_index("pw")
    occ_wide = occupied.astype(jnp.float32).reshape(occupied_count, 1, plane_count, GRID, GRID)
    vir_wide = virtual.astype(jnp.float32).reshape(1, vir_count, plane_count, GRID, GRID)
    density = (occ_wide * vir_wide).reshape(pair_count, plane_count, GRID, GRID)
    counter = jnp.arange(GRID, dtype=jnp.int32)
    cosine_table, sine_table = phase_pair(counter, counter, GRID)
    freq_of_pos = counter % rows_slab * pw_count + counter // rows_slab
    cos_rows, sin_rows = phase_pair(counter, freq_of_pos, GRID)
    forward_z = jnp.concatenate([cosine_table, -sine_table], axis=1)
    field = jnp.dot(density, forward_z, precision=PRECISE)
    field = transform(field, cos_rows, sin_rows, -1.0, "pxyc,yk->pxkc")
    norm_in = 1.0 / math.sqrt(GRID**3)
    freq_x = grid_index // (GRID * GRID)
    freq_y = grid_index // GRID % GRID
    freq_z = grid_index % GRID
    block_g = NG // pw_count
    own_start = slab_pos * block_g
    own_x = lax.dynamic_slice_in_dim(freq_x, own_start, block_g)
    own_y = lax.dynamic_slice_in_dim(freq_y, own_start, block_g)
    own_z = lax.dynamic_slice_in_dim(freq_z, own_start, block_g)
    local_row = (own_x * rows_slab + own_y // pw_count) * (2 * GRID) + own_z

    def finish(pencil):
        eigen_spectrum = transform(pencil, cosine_table, sine_table, -1.0, "pxyc,xk->pkyc")
        flattened = eigen_spectrum.reshape(eigen_spectrum.shape[0], -1)
        real_part = jnp.take(flattened, local_row, axis=1)
        imag_part = jnp.take(flattened, local_row + GRID, axis=1)
        return jnp.stack([real_part, imag_part], axis=1) * norm_in

    eigen_spectra = grouped_exchange(field, "pw", 2, 1, finish, 0, 0)
    rows_here = pair_count * 2
    spectra_low = eigen_spectra.astype(jnp.bfloat16).reshape(rows_here, block_g)
    partial_screened = jnp.dot(
        gathered_copies(spectra_low, "band", 0), screening, preferred_element_type=jnp.float32
    )
    col_block = screening.shape[1]
    arranged = partial_screened.reshape(band_count, rows_here, 1, col_block)
    at_home = lax.all_to_all(arranged, "band", split_axis=0, concat_axis=2, tiled=True)
    whole_cols = at_home.reshape(rows_here, band_count * col_block)
    screened = sent_and_summed(whole_cols, "pw", 1).astype(jnp.bfloat16)
    screened = screened.astype(jnp.float32).reshape(pair_count, 2, block_g)
    pencil = jnp.zeros((pair_count, GRID * rows_slab * 2 * GRID), jnp.float32)
    pencil = pencil.at[:, local_row].set(screened[:, 0]).at[:, local_row + GRID].set(screened[:, 1])
    pencil = pencil.reshape(pair_count, GRID, rows_slab, 2 * GRID)
    pencil = transform(pencil, cosine_table, sine_table, 1.0, "pxyc,xk->pkyc")
    back_z = jnp.concatenate([cosine_table, -sine_table], axis=0)
    norm_out = 1.0 / math.sqrt(NG)
    cos_back = jnp.transpose(cos_rows)
    sin_back = jnp.transpose(sin_rows)
    spatial = transform(
        lax.all_to_all(
            pencil.astype(jnp.bfloat16), "pw", split_axis=1, concat_axis=2, tiled=True
        ).astype(pencil.dtype),
        cos_back,
        sin_back,
        1.0,
        "pxyc,yk->pxkc",
    )
    screened_potential = jnp.dot(spatial, back_z, precision=PRECISE) * norm_out
    screened_potential = screened_potential.reshape(
        occupied_count, vir_count, plane_count, GRID * GRID
    )
    occupied_flat = occupied.astype(jnp.float32)
    return jnp.einsum("qsfz,qfz->sfz", screened_potential, occupied_flat)


def solution(mesh):
    return jax.shard_map(
        body,
        mesh=mesh,
        in_specs=(P(None, "pw", None), P("band", "pw", None), P("pw", "band"), P()),
        out_specs=P("band", "pw", None),
        check_vma=False,
    )
```

profile of v0, /device:TPU:1, one launch (start us, length us, event | category | flops | bytes accessed | tf_op | source)
XLA Modules:
  0.0 254.2 jit_solution(8351152848287864316)
XLA Ops:
  0.2 1.1 reshape.188
  1.3 1.1 reshape.187
  2.4 0.6 fusion.11
  3.0 0.8 convolution_bitcast_fusion.4
  3.8 0.8 convolution_bitcast_fusion.5
  4.5 0.3 fusion.6
  4.9 0.2 pad_maximum_fusion
  5.1 0.9 copy.44
  6.0 10.1 %all-to-all-start.1 = ((f32[1,8,64,128]{3,1,0,2:T(8,128)}), f32[1,8,64,128]{3,1,0,2:T(8,128)S(1)}, u32[]{:S(2)}, u32[]{:S(2)}) async-start(f32[1,8,64,128]{3,1,0,2:T(8,128)} %copy.44), calls=%async_computation.1 | async-start | bytes 524288 | tf_op jit(solution)/shard_map/all_to_all | solution.py:28
  16.1 0.9 broadcast_compare_fusion.1
  17.0 0.9 copy.39
  17.9 0.9 negate_select_fusion.3
  18.8 6.0 %all-to-all-done.1 = f32[1,8,64,128]{3,1,0,2:T(8,128)S(1)} async-done(((f32[1,8,64,128]{3,1,0,2:T(8,128)}), f32[1,8,64,128]{3,1,0,2:T(8,128)S(1)}, u32[]{:S(2)}, u32[]{:S(2)}) %all-to-all-start.1) | async-done | bytes 262176 | tf_op jit(solution)/shard_map/all_to_all | solution.py:28
  24.8 4.4 %all-to-all-start = ((f32[1,8,64,128]{3,1,0,2:T(8,128)}), f32[1,8,64,128]{3,1,0,2:T(8,128)S(1)}, u32[]{:S(2)}, u32[]{:S(2)}) async-start(f32[1,8,64,128]{3,1,0,2:T(8,128)} %copy.39), calls=%async_computation | async-start | bytes 524288 | tf_op jit(solution)/shard_map/all_to_all | solution.py:28
  29.2 0.5 convolution_bitcast_fusion.6
  29.7 0.5 convolution_bitcast_fusion.7
  30.3 7.6 %all-to-all-done = f32[1,8,64,128]{3,1,0,2:T(8,128)S(1)} async-done(((f32[1,8,64,128]{3,1,0,2:T(8,128)}), f32[1,8,64,128]{3,1,0,2:T(8,128)S(1)}, u32[]{:S(2)}, u32[]{:S(2)}) %all-to-all-start) | async-done | bytes 262176 | tf_op jit(solution)/shard_map/all_to_all | solution.py:28
  37.9 0.5 convolution_bitcast_fusion.8
  38.4 0.5 convolution_bitcast_fusion.9
  39.0 0.2 fusion.15
  39.3 0.2 copy.119
  39.5 11.8 %gather_fusion.3 = f32[2048]{0:T(1024)S(1)} fusion(f32[65536]{0:T(1024)S(1)} %bitcast.148, s32[2048]{0:T(1024)S(1)} %get-tuple-element.37), kind=kCustom, calls=%fused_computation.3.clone | custom fusion | bytes 24576 | tf_op jit(solution)/shard_map/jit(_take)/gather | solution.py:114
  51.3 11.8 %gather_fusion.2 = f32[2048]{0:T(1024)S(1)} fusion(f32[65536]{0:T(1024)S(1)} %bitcast.149, s32[2048]{0:T(1024)S(1)} %get-tuple-element.35), kind=kCustom, calls=%fused_computation.2.clone | custom fusion | bytes 24576 | tf_op jit(solution)/shard_map/jit(_take)/gather | solution.py:113
  63.1 0.2 fusion.17
  63.6 11.8 %gather_fusion.1 = f32[2048]{0:T(1024)S(1)} fusion(f32[65536]{0:T(1024)S(1)} %bitcast.146, s32[2048]{0:T(1024)S(1)} %get-tuple-element.37), kind=kCustom, calls=%fused_computation.1.clone | custom fusion | bytes 24576 | tf_op jit(solution)/shard_map/jit(_take)/gather | solution.py:114
  75.4 11.8 %gather_fusion = f32[2048]{0:T(1024)S(1)} fusion(f32[65536]{0:T(1024)S(1)} %bitcast.147, s32[2048]{0:T(1024)S(1)} %get-tuple-element.35), kind=kCustom, calls=%fused_computation.clone | custom fusion | bytes 24576 | tf_op jit(solution)/shard_map/jit(_take)/gather | solution.py:113
  87.3 0.5 broadcast_in_dim.27
  87.8 45.2 %all_to_all.73 = bf16[64,4,2048]{2,1,0:T(4,128)(2,1)S(1)} all-to-all(bf16[64,4,2048]{2,1,0:T(4,128)(2,1)S(1)} %broadcast_in_dim.27), channel_id=1, replica_groups=mesh['band'=64,'pw'=8] {'band'}, dimensions={0} | all-to-all | bytes 2097152 | tf_op jit(solution)/shard_map/all_to_all | solution.py:38
  133.0 1.3 convolution_bitcast_fusion.10
  134.2 0.2 copy.50
  134.4 21.2 %all_to_all.74 = f32[64,4,1,256]{3,1,2,0:T(4,128)S(1)} all-to-all(f32[64,4,1,256]{3,1,2,0:T(4,128)S(1)} %copy.50), channel_id=1, replica_groups=mesh['band'=64,'pw'=8] {'band'}, dimensions={0} | all-to-all | bytes 524288 | tf_op jit(solution)/shard_map/all_to_all | solution.py:125
  155.6 15.1 %all_to_all.75 = f32[8,4,2048]{2,1,0:T(4,128)S(1)} all-to-all(f32[8,4,2048]{2,1,0:T(4,128)S(1)} %bitcast.157), channel_id=1, replica_groups=mesh['band'=64,'pw'=8] {'pw'}, dimensions={0} | all-to-all | bytes 524288 | tf_op jit(solution)/shard_map/all_to_all | solution.py:61
  170.8 0.4 copy.51
  171.2 0.4 copy.52
  171.6 18.8 %scatter_custom_fusion = f32[2,65536]{0,1:T(8,128)} fusion(s32[2048]{0:T(1024)S(1)} %get-tuple-element.36, f32[2048,2]{1,0:T(8,128)S(1)} %copy.51, f32[]{:T(128)} %constant.122.clone.1), kind=kCustom, calls=%fused_computation.6 | custom fusion | bytes 524292 | tf_op jit(solution)/shard_map/scatter | solution.py:130
  190.3 27.1 %scatter_fusion = f32[2,65536]{0,1:T(8,128)} fusion(f32[2,65536]{0,1:T(8,128)} %scatter_custom_fusion, s32[2048]{0:T(1024)S(1)} %get-tuple-element.6, f32[2048,2]{1,0:T(8,128)S(1)} %copy.52), kind=kCustom, calls=%fused_computation.5 | custom fusion | bytes 57344 | tf_op jit(solution)/shard_map/scatter | solution.py:130
  217.5 19.5 %copy.54 = f32[2,64,8,128]{3,1,2,0:T(8,128)S(1)} copy(f32[2,64,8,128]{0,3,2,1:T(8,128)} %bitcast.150) | data formatting | bytes 1048576 | tf_op jit(solution)/shard_map/reshape | solution.py:131
  237.0 0.8 convolution_bitcast_fusion.2
  237.8 0.8 convolution_bitcast_fusion.3
  238.5 0.3 fusion.5
  239.0 0.2 copy.57
  239.2 12.1 %all_to_all.76 = bf16[2,64,8,128]{3,2,0,1:T(8,128)(2,1)S(1)} all-to-all(bf16[2,64,8,128]{3,2,0,1:T(8,128)(2,1)S(1)} %copy.57), channel_id=1, replica_groups=mesh['band'=64,'pw'=8] {'pw'}, dimensions={1} | all-to-all | bytes 524288 | tf_op jit(solution)/shard_map/all_to_all | solution.py:138
  251.3 0.5 convolution_bitcast_fusion
  251.8 0.5 convolution_bitcast_fusion.1
  252.3 0.3 slice_subtract_fusion
  252.6 0.6 convolution_multiply_fusion
  253.3 0.2 reshape.185
  253.5 0.7 multiply_reduce_fusion
  (24 shorter events, 1.0 us)
Async XLA Ops:
  0.0 133.0 %copy-start = (bf16[2048,256]{1,0:T(8,128)(2,1)S(1)}, bf16[2048,256]{1,0:T(8,128)(2,1)}, u32[]{:S(2)}) copy-start(bf16[2048,256]{1,0:T(8,128)(2,1)} %param.8) | copy-start | bytes 3145732
  6.0 18.8 %all-to-all-start.1 = ((f32[1,8,64,128]{3,1,0,2:T(8,128)}), f32[1,8,64,128]{3,1,0,2:T(8,128)S(1)}, u32[]{:S(2)}, u32[]{:S(2)}) async-start(f32[1,8,64,128]{3,1,0,2:T(8,128)} %copy.44), calls=%async_computation.1 | async-start | bytes 524288 | tf_op jit(solution)/shard_map/all_to_all | solution.py:28
  24.8 13.1 %all-to-all-start = ((f32[1,8,64,128]{3,1,0,2:T(8,128)}), f32[1,8,64,128]{3,1,0,2:T(8,128)S(1)}, u32[]{:S(2)}, u32[]{:S(2)}) async-start(f32[1,8,64,128]{3,1,0,2:T(8,128)} %copy.39), calls=%async_computation | async-start | bytes 524288 | tf_op jit(solution)/shard_map/all_to_all | solution.py:28
  171.6 81.9 %copy-start.1 = (bf16[2,8,4096]{2,1,0:T(8,128)(2,1)S(1)}, bf16[2,8,4096]{2,1,0:T(8,128)(2,1)}, u32[]{:S(2)}) copy-start(bf16[2,8,4096]{2,1,0:T(8,128)(2,1)} %param.6) | copy-start | bytes 393220
where the time goes:
time: 255 us; the launch traced here: 254 us
  local copies, waits for them, and re-layouts  119 us (47%)
  blocking collectives  93.5 us (37%)
  starting transfers between devices  14.5 us (6%)
  waiting for transfers between devices  13.6 us (5%)
  matrix products  8.68 us (3%)
  other arithmetic  4.86 us (2%)
    scatter x2, local copies, waits for them, and re-layouts, body(): pencil.at[:, local_row].set(screened[:, 0]).at[:, local_row + GRID]  45.9 us
    all_to_all x1, blocking collectives, from_everyone(): lax.all_to_all(jnp.broadcast_to(array[None], (devices, *array.shape)), ax...  45.2 us
    gather x2, local copies, waits for them, and re-layouts, finish(): imag_part = jnp.take(flattened, local_row + GRID, axis=1)  23.6 us
    gather x2, local copies, waits for them, and re-layouts, finish(): real_part = jnp.take(flattened, local_row, axis=1)  23.6 us
    all_to_all x1, blocking collectives, body(): lax.all_to_all(arranged, 'band', split_axis=0, concat_axis=2, tiled=True)  21.2 us
    reshape x1, local copies, waits for them, and re-layouts, body(): pencil = pencil.reshape(pair_count, GRID, rows_slab, 2 * GRID)  19.5 us
    all_to_all x1, blocking collectives, sent_and_summed(): lax.all_to_all(in_blocks(array, dim, devices), axis, 0, 0, tiled=True)  15.1 us
    all_to_all x2, starting transfers between devices, grouped_exchange(): lax.all_to_all(group, axis, split_axis=split_dim, concat_axis=concat_dim,...  14.5 us
  transfers between devices with their start and end apart: 2, of which 2 were waited for; matrix products, arithmetic and copies ran while one was open for 1% of the time, Pallas kernels for 0%

commit v1 on v0

v1 whole, which is shorter than its diff:
```python
import math

import jax
import jax.numpy as jnp
from jax import lax
from jax.sharding import PartitionSpec as P

GRID = 64
NG = 16384
KMAX = 16
NK = 2 * KMAX + 1
PW = 8
BAND = 64
NJ = 5
PRECISE = lax.Precision.HIGHEST
F32 = jnp.float32
BF16 = jnp.bfloat16


def phases(left, right):
    angles = (left[:, None] * right[None, :] % GRID).astype(F32) * (2.0 * math.pi / GRID)
    return jnp.cos(angles), jnp.sin(angles)


def dot(spec, a, b):
    return jnp.einsum(spec, a, b, precision=PRECISE, preferred_element_type=F32)


def body(occupied, virtual, screening, grid_index):
    pairs, planes = occupied.shape[0], occupied.shape[1]
    slab = lax.axis_index("pw")
    cells = jnp.arange(GRID, dtype=jnp.int32)
    freqs = jnp.arange(NK, dtype=jnp.int32) - KMAX
    row_freqs = jnp.arange(PW, dtype=jnp.int32)[:, None] - KMAX + PW * jnp.arange(NJ, dtype=jnp.int32)[None]
    cos_k, sin_k = phases(cells, freqs)
    cos_y, sin_y = phases(cells, row_freqs.reshape(-1))

    block = NG // PW
    own = lax.dynamic_slice_in_dim(grid_index, slab * block, block)

    def signed(k):
        return jnp.where(k >= GRID // 2, k - GRID, k)

    at_x = signed(own // (GRID * GRID)) + KMAX
    at_j = (signed(own // GRID % GRID) + KMAX - slab) // PW
    at_z = signed(own % GRID) + KMAX
    at_jz = at_j * NK + at_z
    pick_x = (jnp.arange(NK, dtype=jnp.int32)[:, None] == at_x[None]).astype(BF16)
    pick_jz = jnp.arange(NJ * NK, dtype=jnp.int32)[:, None] == at_jz[None]

    density = occupied.astype(F32) * virtual.astype(F32)
    density = density.reshape(pairs, planes, GRID, GRID)
    forward_z = jnp.concatenate([cos_k, -sin_k], axis=1)
    field = dot("pxyz,zc->pxyc", density, forward_z)
    both_y = jnp.concatenate([cos_y, sin_y], axis=1)
    mixed = dot("pxyc,yk->pxkc", field, both_y).reshape(pairs, planes, 2, PW, NJ, 2, NK)
    real = mixed[:, :, 0, :, :, 0] + mixed[:, :, 1, :, :, 1]
    imag = mixed[:, :, 0, :, :, 1] - mixed[:, :, 1, :, :, 0]
    field = jnp.stack([real, imag], axis=0).astype(BF16)
    field = field.transpose(3, 2, 1, 0, 4, 5).reshape(PW, planes, pairs * 2 * NJ * NK)
    pencil = lax.all_to_all(field, "pw", 0, 0, tiled=True).reshape(GRID, -1)

    cos_sin = jnp.concatenate([cos_k, sin_k], axis=1)
    mixed = dot("xm,xk->mk", pencil.astype(F32), cos_sin).reshape(pairs, 2, NJ * NK, 2, NK)
    real = mixed[:, 0, :, 0] + mixed[:, 1, :, 1]
    imag = mixed[:, 1, :, 0] - mixed[:, 0, :, 1]
    box = (jnp.stack([real, imag], axis=1) * (1.0 / math.sqrt(GRID**3))).astype(BF16)
    columns = jnp.einsum("prmk,kg->prmg", box, pick_x, preferred_element_type=F32)
    spectra = jnp.sum(jnp.where(pick_jz[None, None], columns, 0.0), axis=2).astype(BF16)

    rows = pairs * 2
    everyone = lax.all_gather(spectra.reshape(rows, block), "band", axis=0, tiled=True)
    partial = jnp.dot(everyone, screening, preferred_element_type=F32).astype(BF16)

    width = screening.shape[1]
    partial = lax.all_to_all(partial.reshape(PW, PW * rows, width), "pw", 0, 0, tiled=True)
    summed = jnp.sum(partial.astype(F32), axis=0).astype(BF16).reshape(PW, rows, width)
    turn = []
    for c1 in range(PW):
        for c0 in range(PW):
            for p in range(PW):
                turn.append(((c1 * PW + c0) * PW + p, (p * PW + c0) * PW + c1))
    summed = lax.ppermute(summed, ("band", "pw"), turn)
    groups = [[PW * k + t for t in range(PW)] for k in range(BAND // PW)]
    home = lax.all_to_all(summed, "band", 0, 0, axis_index_groups=groups, tiled=True)
    screened = home.transpose(1, 0, 2).reshape(rows, 1, block)

    spread = jnp.where(pick_jz[None], screened, jnp.zeros((), BF16)).reshape(rows * NJ * NK, block)
    box = jnp.einsum("mg,kg->mk", spread, pick_x, preferred_element_type=F32)
    mixed = dot("xk,mk->xm", jnp.concatenate([cos_k, sin_k], axis=0), box)
    mixed = mixed.reshape(2, GRID, pairs, 2, NJ * NK)
    real = mixed[0, :, :, 0] - mixed[1, :, :, 1]
    imag = mixed[0, :, :, 1] + mixed[1, :, :, 0]
    pencil = jnp.stack([real, imag], axis=2).astype(BF16).reshape(PW, planes, -1)
    field = lax.all_to_all(pencil, "pw", 0, 0, tiled=True)
    field = field.reshape(PW, planes, pairs, 2, NJ, NK).astype(F32)
    field = field.transpose(2, 1, 0, 4, 3, 5).reshape(pairs, planes, PW * NJ, 2 * NK)
    mixed = dot("pxkc,yk->pxyc", field, jnp.concatenate([cos_y, sin_y], axis=0))
    mixed = mixed.reshape(pairs, planes, 2, GRID, 2 * NK)
    mixed = jnp.concatenate([mixed[:, :, 0], mixed[:, :, 1]], axis=-1)
    cz, sz = jnp.transpose(cos_k), jnp.transpose(sin_k)
    back = jnp.concatenate([cz, -sz, -sz, -cz], axis=0) * (1.0 / math.sqrt(NG))
    potential = dot("pxyc,cz->pxyz", mixed, back)
    weighted = potential.reshape(pairs, planes, GRID * GRID) * occupied.astype(F32)
    return jnp.sum(weighted, axis=0)[None]


def solution(mesh):
    return jax.shard_map(
        body,
        mesh=mesh,
        in_specs=(P(None, "pw", None), P("band", "pw", None), P("pw", "band"), P()),
        out_specs=P("band", "pw", None),
        check_vma=False,
    )
```

time: 255 us -> 235 us (0.922)
  waiting for transfers between devices: 13.6 us -> 140 us
  local copies, waits for them, and re-layouts: 119 us -> 15.7 us
  blocking collectives: 93.5 us -> 26.3 us
  between operations: 0.36 us -> 13.7 us
  starting transfers between devices: 14.5 us -> 22.9 us
    all_gather x0 -> x1, waiting for transfers between devices: none -> 127 us  [body(): lax.all_gather(spectra.reshape(rows, block), 'band', axis=0, tiled=True)]
    all_to_all x4 -> x2, blocking collectives: 93.5 us -> 26.3 us  [the longest x1 13.9 us: body(): lax.all_to_all(partial.reshape(PW, PW * rows, width), 'pw', 0, 0, tiled=T...]
    gather x4 -> x0, local copies, waits for them, and re-layouts: 47.1 us -> none  [the longest x2 23.6 us: finish(): imag_part = jnp.take(flattened, local_row + GRID, axis=1)]
    scatter x2 -> x0, local copies, waits for them, and re-layouts: 45.9 us -> none  [body(): pencil.at[:, local_row].set(screened[:, 0]).at[:, local_row + GRID]]
    reshape x2 -> x9, local copies, waits for them, and re-layouts: 20.6 us -> 4.89 us  [the longest x1 1.2 us: body(): field.transpose(3, 2, 1, 0, 4, 5).reshape(PW, planes, pairs * 2 * NJ * NK)]
    ppermute x0 -> x1, starting transfers between devices: none -> 4.9 us  [body(): summed = lax.ppermute(summed, ('band', 'pw'), turn)]
    all_to_all x2, waiting for transfers between devices: 13.6 us -> 8.93 us  [the longest x1 5.21 us: body(): field = lax.all_to_all(pencil, 'pw', 0, 0, tiled=True)]
    select_n x0 -> x1, local copies, waits for them, and re-layouts: none -> 4.06 us  [body(): jnp.where(pick_jz[None], screened, jnp.zeros((), BF16))]
  transfers between devices with their start and end apart: 2 -> 4, of which waited for: 2 -> 4; matrix products, arithmetic and copies ran while one was open for 1% -> 1% of each run, Pallas kernels for 0% -> 0%
where the time goes in v1:
time: 235 us; the launch traced here: 234 us
  waiting for transfers between devices  140 us (60%)
  blocking collectives  26.3 us (11%)
  starting transfers between devices  22.9 us (10%)
  local copies, waits for them, and re-layouts  15.7 us (7%)
  between operations  13.7 us (6%)
  matrix products  8.27 us (4%)
  other arithmetic  7 us (3%)
    all_gather x1, waiting for transfers between devices, body(): lax.all_gather(spectra.reshape(rows, block), 'band', axis=0, tiled=True)  127 us
    all_to_all x1, blocking collectives, body(): lax.all_to_all(partial.reshape(PW, PW * rows, width), 'pw', 0, 0, tiled=T...  13.9 us
    all_to_all x1, blocking collectives, body(): lax.all_to_all(summed, 'band', 0, 0, axis_index_groups=groups, tiled=True)  12.4 us
    all_to_all x1, starting transfers between devices, body(): pencil = lax.all_to_all(field, 'pw', 0, 0, tiled=True).reshape(GRID, -1)  10.1 us
    all_to_all x1, starting transfers between devices, body(): field = lax.all_to_all(pencil, 'pw', 0, 0, tiled=True)  7.91 us
    all_to_all x1, waiting for transfers between devices, body(): field = lax.all_to_all(pencil, 'pw', 0, 0, tiled=True)  5.21 us
    ppermute x1, starting transfers between devices, body(): summed = lax.ppermute(summed, ('band', 'pw'), turn)  4.9 us
  transfers between devices with their start and end apart: 4, of which 4 were waited for; matrix products, arithmetic and copies ran while one was open for 1% of the time, Pallas kernels for 0%

profile of v1, /device:TPU:1, one launch (start us, length us, event | category | flops | bytes accessed | tf_op | source)
XLA Modules:
  0.0 234.0 jit_solution(1686862326288065486)
XLA Ops:
  6.5 0.2 fusion.68
  6.7 0.9 bitcast_convert_fusion
  7.7 0.9 convert_multiply_fusion.1
  8.6 0.2 reshape.230
  9.0 0.2 fusion.71
  9.2 0.6 fusion.37
  9.7 1.1 convolution_bitcast_fusion.1
  10.9 0.3 copy.91
  11.1 0.8 reshape.231
  11.9 1.0 fusion.90
  13.2 1.2 reshape.232
  14.4 10.1 %all-to-all-start = ((bf16[8,8,660]{2,1,0:T(8,128)(2,1)}), bf16[8,8,660]{2,1,0:T(8,128)(2,1)S(1)}, u32[]{:S(2)}, u32[]{:S(2)}) async-start(bf16[8,8,660]{2,1,0:T(8,128)(2,1)} %reshape.232), calls=%async_computation | async-start | bytes 196608 | tf_op jit(solution)/shard_map/all_to_all | solution.py:61
  24.5 0.7 fusion.80
  25.2 0.7 fusion.75
  25.9 0.2 iota_compare_fusion
  26.2 3.7 %all-to-all-done = bf16[8,8,660]{2,1,0:T(8,128)(2,1)S(1)} async-done(((bf16[8,8,660]{2,1,0:T(8,128)(2,1)}), bf16[8,8,660]{2,1,0:T(8,128)(2,1)S(1)}, u32[]{:S(2)}, u32[]{:S(2)}) %all-to-all-start) | async-done | bytes 84512 | tf_op jit(solution)/shard_map/all_to_all | solution.py:61
  29.9 0.1 dot_general.38
  30.0 0.3 fusion.17
  30.4 1.0 select_reduce_fusion
  31.4 0.6 reshape.242
  32.0 127.1 %all-gather.3.cloned.1.call-done = bf16[64,4,2048]{2,1,0:T(4,128)(2,1)} async-done(((bf16[1,4,2048]{2,1,0:T(4,128)(2,1)}), bf16[64,4,2048]{2,1,0:T(4,128)(2,1)}) %all-gather.3.cloned.1.call-update) | async-done | bytes 1048592 | tf_op jit(solution)/shard_map/all_gather | solution.py:72
  159.1 1.3 reshape.243
  160.5 0.4 convolution_convert_fusion
  160.9 13.9 %all_to_all.20 = bf16[8,32,256]{2,1,0:T(8,128)(2,1)S(1)} all-to-all(bf16[8,32,256]{2,1,0:T(8,128)(2,1)S(1)} %bitcast.87), channel_id=1, replica_groups=mesh['band'=64,'pw'=8] {'pw'}, dimensions={0} | all-to-all | bytes 262144 | tf_op jit(solution)/shard_map/all_to_all | solution.py:76
  174.9 4.9 %collective-permute-start = (bf16[8,4,256]{2,1,0:T(4,128)(2,1)S(1)}, bf16[8,4,256]{2,1,0:T(4,128)(2,1)S(1)}, u32[]{:S(2)}, u32[]{:S(2)}) collective-permute-start(bf16[8,4,256]{2,1,0:T(4,128)(2,1)S(1)} %reshape.235), channel_id=1, source_target_pairs={{0,0},{1,64},{2,128},{3,192},{4,256},{5,320},{6,384},{7,448},{8,8}... | collective-permute-start | bytes 49160 | tf_op jit(solution)/shard_map/ppermute | solution.py:83
  179.8 4.1 %collective-permute-done = bf16[8,4,256]{2,1,0:T(4,128)(2,1)S(1)} collective-permute-done((bf16[8,4,256]{2,1,0:T(4,128)(2,1)S(1)}, bf16[8,4,256]{2,1,0:T(4,128)(2,1)S(1)}, u32[]{:S(2)}, u32[]{:S(2)}) %collective-permute-start) | collective-permute-done | bytes 16416 | tf_op jit(solution)/shard_map/ppermute | solution.py:83
  183.8 12.4 %all_to_all.21 = bf16[8,4,256]{2,1,0:T(4,128)(2,1)S(1)} all-to-all(bf16[8,4,256]{2,1,0:T(4,128)(2,1)S(1)} %collective-permute-done), channel_id=1, replica_groups={{0,8,16,24,32,40,48,56},{64,72,80,88,96,104,112,120},{128,136,144,152,1..., dimensions={0} | all-to-all | bytes 32768 | tf_op jit(solution)/shard_map/all_to_all | solution.py:85
  196.3 2.0 broadcast_select_fusion
  198.2 4.1 %select_n.97 = bf16[660,2048]{1,0:T(8,128)(2,1)} reshape(bf16[4,165,2048]{2,1,0:T(8,128)(2,1)} %broadcast_select_fusion) | data formatting | bytes 5406720 | tf_op jit(solution)/shard_map/jit(_where)/select_n | solution.py:88
  202.3 2.7 %fusion.6 = f32[660,33]{0,1:T(8,128)S(1)} fusion(bf16[660,2048]{1,0:T(8,128)(2,1)} %select_n.97, s32[2048]{0:T(1024)S(1)} %get-tuple-element.5), kind=kOutput, calls=%fused_computation.18 | convolution fusion | flops 89278464 | bytes 2798672 | tf_op jit(solution)/shard_map/mg,kg->mk/dot_general | solution.py:89
  205.0 0.6 fusion.56
  205.6 0.8 reshape.236
  206.4 0.4 fusion.92
  207.0 0.8 convert_element_type.68
  207.8 7.9 %all-to-all-start.3 = ((bf16[8,8,660]{2,1,0:T(8,128)(2,1)}), bf16[8,8,660]{2,1,0:T(8,128)(2,1)S(1)}, u32[]{:S(2)}, u32[]{:S(2)}) async-start(bf16[8,8,660]{2,1,0:T(8,128)(2,1)} %convert_element_type.68), calls=%async_computation.3 | async-start | bytes 196608 | tf_op jit(solution)/shard_map/all_to_all | solution.py:95
  215.7 0.2 fusion.66
  215.9 5.2 %all-to-all-done.3 = bf16[8,8,660]{2,1,0:T(8,128)(2,1)S(1)} async-done(((bf16[8,8,660]{2,1,0:T(8,128)(2,1)}), bf16[8,8,660]{2,1,0:T(8,128)(2,1)S(1)}, u32[]{:S(2)}, u32[]{:S(2)}) %all-to-all-start.3) | async-done | bytes 84512 | tf_op jit(solution)/shard_map/all_to_all | solution.py:95
  221.1 0.9 reshape.237
  222.0 0.3 copy.107
  222.3 0.2 reshape.238
  222.5 0.5 convolution_bitcast_fusion
  223.0 0.6 reshape.253
  223.6 0.8 fusion.91
  224.4 0.4 copy.135
  224.8 0.4 copy.136
  225.2 1.1 fusion
  226.3 0.2 reshape.240
  226.5 0.7 fusion.9
  (24 shorter events, 0.7 us)
Async XLA Ops:
  6.5 153.9 %copy-start = (bf16[2048,256]{1,0:T(8,128)(2,1)S(1)}, bf16[2048,256]{1,0:T(8,128)(2,1)}, u32[]{:S(2)}) copy-start(bf16[2048,256]{1,0:T(8,128)(2,1)} %param.6) | copy-start | bytes 3145732
  14.4 15.5 %all-to-all-start = ((bf16[8,8,660]{2,1,0:T(8,128)(2,1)}), bf16[8,8,660]{2,1,0:T(8,128)(2,1)S(1)}, u32[]{:S(2)}, u32[]{:S(2)}) async-start(bf16[8,8,660]{2,1,0:T(8,128)(2,1)} %reshape.232), calls=%async_computation | async-start | bytes 196608 | tf_op jit(solution)/shard_map/all_to_all | solution.py:61
  24.5 134.6 %all-gather.3.cloned.1.call-start = ((), (), s32[]{:S(2)}) async-start(), calls=%async_computation.4 | async-start | bytes 1064960 | tf_op jit(solution)/shard_map/all_gather | solution.py:72
  174.9 9.0 %collective-permute-start = (bf16[8,4,256]{2,1,0:T(4,128)(2,1)S(1)}, bf16[8,4,256]{2,1,0:T(4,128)(2,1)S(1)}, u32[]{:S(2)}, u32[]{:S(2)}) collective-permute-start(bf16[8,4,256]{2,1,0:T(4,128)(2,1)S(1)} %reshape.235), channel_id=1, source_target_pairs={{0,0},{1,64},{2,128},{3,192},{4,256},{5,320},{6,384},{7,448},{8,8}... | collective-permute-start | bytes 49160 | tf_op jit(solution)/shard_map/ppermute | solution.py:83
  207.8 13.3 %all-to-all-start.3 = ((bf16[8,8,660]{2,1,0:T(8,128)(2,1)}), bf16[8,8,660]{2,1,0:T(8,128)(2,1)S(1)}, u32[]{:S(2)}, u32[]{:S(2)}) async-start(bf16[8,8,660]{2,1,0:T(8,128)(2,1)} %convert_element_type.68), calls=%async_computation.3 | async-start | bytes 196608 | tf_op jit(solution)/shard_map/all_to_all | solution.py:95
  224.4 2.1 copy-start.1
Sparse Core Ops, SparseCore 0:
  32.2 126.9 all-gather.2

commit v2 on v1

--- a/solution.py
+++ b/solution.py
@@ -3,6 +3,8 @@
 import jax
 import jax.numpy as jnp
 from jax import lax
+from jax.experimental import pallas as pl
+from jax.experimental.pallas import tpu as pltpu
 from jax.sharding import PartitionSpec as P
 
 GRID = 64
@@ -24,6 +26,172 @@
 
 def dot(spec, a, b):
     return jnp.einsum(spec, a, b, precision=PRECISE, preferred_element_type=F32)
+
+
+MESH = pl.DeviceIdType.MESH
+
+
+def remote(src, dst, send, recv, device):
+    return pltpu.make_async_remote_copy(
+        src_ref=src, dst_ref=dst, send_sem=send, recv_sem=recv, device_id=device, device_id_type=MESH
+    )
+
+
+def greet(devices, count):
+    barrier = pltpu.get_barrier_semaphore()
+    for device in devices:
+        pl.semaphore_signal(barrier, inc=1, device_id=device, device_id_type=MESH)
+    pl.semaphore_wait(barrier, count)
+
+
+OFFSETS = (1, 7, 2, 6, 3, 5, 4)
+
+
+def gather_kernel(own_ref, all_ref, own_sem, z_sems, ys_sems, yr_sems, xs_sems, xr_sems, fs_sems, fr_sems):
+    band, pw = lax.axis_index("band"), lax.axis_index("pw")
+    x, y, z = band // 16, lax.rem(band // 2, 8), lax.rem(band, 2)
+
+    def at(x_at, y_at, z_at):
+        return (x_at * 16 + y_at * 2 + z_at, pw)
+
+    def up(d):
+        return lax.rem(y + d, 8)
+
+    right, left = lax.rem(x + 1, 4), lax.rem(x + 3, 4)
+    across = at(x, y, 1 - z)
+    beside = (at(right, y, z), at(left, y, z))
+    greet([across, *beside, *[at(x, up(d), z) for d in OFFSETS]], 3 + len(OFFSETS))
+
+    keep = pltpu.make_async_copy(own_ref, all_ref.at[x, y, z], own_sem)
+    keep.start()
+    to_across = remote(own_ref, all_ref.at[x, y, z], z_sems.at[0], z_sems.at[1], across)
+    to_across.start()
+    y_copies = {}
+    for d in OFFSETS:
+        y_copies[0, d] = remote(
+            own_ref, all_ref.at[x, y, z], ys_sems.at[0, d], yr_sems.at[0, d], at(x, up(d), z)
+        )
+        y_copies[0, d].start()
+    to_across.wait_recv()
+    other = all_ref.at[x, y, 1 - z]
+    for d in OFFSETS:
+        y_copies[1, d] = remote(other, other, ys_sems.at[1, d], yr_sems.at[1, d], at(x, up(d), z))
+        y_copies[1, d].start()
+    keep.wait()
+    order = (0,) + OFFSETS
+    x_copies = []
+    for k, d in enumerate(order):
+        if d:
+            y_copies[0, d].wait_recv()
+            y_copies[1, d].wait_recv()
+        piece = all_ref.at[x, lax.rem(y + 8 - d, 8)]
+        for side in range(2):
+            copy = remote(piece, piece, xs_sems.at[side, k], xr_sems.at[side, k], beside[side])
+            copy.start()
+            x_copies.append(copy)
+    forwards = []
+    for k, d in enumerate(order):
+        first = k % 2
+        for side in (first, 1 - first):
+            x_copies[2 * k + side].wait_recv()
+            if side == first:
+                source = left if side == 0 else right
+                piece = all_ref.at[source, lax.rem(y + 8 - d, 8)]
+                copy = remote(piece, piece, fs_sems.at[k], fr_sems.at[k], beside[side])
+                copy.start()
+                forwards.append(copy)
+    for copy in forwards:
+        copy.wait_recv()
+    to_across.wait_send()
+    for copy in [*y_copies.values(), *x_copies, *forwards]:
+        copy.wait_send()
+
+
+def gathered(own):
+    dma = pltpu.SemaphoreType.DMA
+    return pl.pallas_call(
+        gather_kernel,
+        out_shape=jax.ShapeDtypeStruct((4, 8, 2, *own.shape), own.dtype),
+        in_specs=[pl.BlockSpec(memory_space=pltpu.VMEM)],
+        out_specs=pl.BlockSpec(memory_space=pltpu.VMEM),
+        scratch_shapes=[
+            dma, dma((2,)), dma((2, 8)), dma((2, 8)), dma((2, 8)), dma((2, 8)), dma((8,)), dma((8,))
+        ],
+        compiler_params=pltpu.CompilerParams(collective_id=0, has_side_effects=True),
+    )(own)
+
+
+def home_kernel(part_ref, home_ref, landed, summed, ps_sems, pr_sems, cs_sems, cr_sems, own_sem):
+    band, pw = lax.axis_index("band"), lax.axis_index("pw")
+    high, low = band // PW, lax.rem(band, PW)
+    same = high == pw
+
+    def over(d):
+        return lax.rem(pw + d, PW)
+
+    barrier = pltpu.get_barrier_semaphore()
+    for d in range(1, PW):
+        pl.semaphore_signal(barrier, inc=1, device_id=(band, over(d)), device_id_type=MESH)
+    for t in range(PW):
+        @pl.when(jnp.logical_not(same & (low == t)))
+        def _():
+            pl.semaphore_signal(barrier, inc=1, device_id=(pw * PW + t, high), device_id_type=MESH)
+    pl.semaphore_wait(barrier, jnp.where(same, 2 * PW - 2, 2 * PW - 1))
+
+    copies = []
+    for d in range(1, PW):
+        copy = remote(part_ref.at[over(d)], landed.at[pw], ps_sems.at[d], pr_sems.at[d], (band, over(d)))
+        copy.start()
+        copies.append(copy)
+    total = part_ref[pw].astype(F32)
+    for d in range(1, PW):
+        copies[d - 1].wait_recv()
+        total = total + landed[lax.rem(pw + PW - d, PW)].astype(F32)
+    rows = total.shape[0] // PW
+    for t in range(PW):
+        summed[t] = total[t * rows : (t + 1) * rows]
+
+    def across(t, sem):
+        return remote(summed.at[t], home_ref.at[low], cs_sems.at[t], cr_sems.at[sem], (pw * PW + t, high))
+
+    for t in range(PW):
+        mine = same & (low == t)
+
+        @pl.when(mine)
+        def _():
+            own = pltpu.make_async_copy(summed.at[t], home_ref.at[low], own_sem)
+            own.start()
+            own.wait()
+
+        @pl.when(jnp.logical_not(mine))
+        def _():
+            across(t, low).start()
+
+    for t in range(PW):
+        @pl.when(jnp.logical_not(same & (low == t)))
+        def _():
+            pltpu.make_async_remote_copy(
+                src_ref=summed.at[t], dst_ref=home_ref.at[t], send_sem=cs_sems.at[t],
+                recv_sem=cr_sems.at[t], device_id=(pw * PW + t, high), device_id_type=MESH,
+            ).wait()
+    for copy in copies:
+        copy.wait_send()
+
+
+def brought_home(partial):
+    dma = pltpu.SemaphoreType.DMA
+    rows, width = partial.shape[1] // PW, partial.shape[2]
+    return pl.pallas_call(
+        home_kernel,
+        out_shape=jax.ShapeDtypeStruct((PW, rows, width), F32),
+        in_specs=[pl.BlockSpec(memory_space=pltpu.VMEM)],
+        out_specs=pl.BlockSpec(memory_space=pltpu.VMEM),
+        scratch_shapes=[
+            pltpu.VMEM(partial.shape, BF16), pltpu.VMEM((PW, rows, width), F32),
+            dma((PW,)), dma((PW,)), dma((PW,)), dma((PW,)), dma,
+        ],
+        compiler_params=pltpu.CompilerParams(collective_id=1, has_side_effects=True),
+    )(partial)
 
 
 def body(occupied, virtual, screening, grid_index):
@@ -65,29 +233,21 @@
     real = mixed[:, 0, :, 0] + mixed[:, 1, :, 1]
     imag = mixed[:, 1, :, 0] - mixed[:, 0, :, 1]
     box = (jnp.stack([real, imag], axis=1) * (1.0 / math.sqrt(GRID**3))).astype(BF16)
-    columns = jnp.einsum("prmk,kg->prmg", box, pick_x, preferred_element_type=F32)
-    spectra = jnp.sum(jnp.where(pick_jz[None, None], columns, 0.0), axis=2).astype(BF16)
+    columns = jnp.einsum("prmk,mg->prkg", box, pick_jz.astype(BF16), preferred_element_type=F32)
+    spectra = jnp.sum(columns * pick_x.astype(F32), axis=2).astype(BF16)
 
     rows = pairs * 2
-    everyone = lax.all_gather(spectra.reshape(rows, block), "band", axis=0, tiled=True)
+    everyone = gathered(spectra.reshape(rows, block)).reshape(BAND * rows, block)
     partial = jnp.dot(everyone, screening, preferred_element_type=F32).astype(BF16)
 
     width = screening.shape[1]
-    partial = lax.all_to_all(partial.reshape(PW, PW * rows, width), "pw", 0, 0, tiled=True)
-    summed = jnp.sum(partial.astype(F32), axis=0).astype(BF16).reshape(PW, rows, width)
-    turn = []
-    for c1 in range(PW):
-        for c0 in range(PW):
-            for p in range(PW):
-                turn.append(((c1 * PW + c0) * PW + p, (p * PW + c0) * PW + c1))
-    summed = lax.ppermute(summed, ("band", "pw"), turn)
-    groups = [[PW * k + t for t in range(PW)] for k in range(BAND // PW)]
-    home = lax.all_to_all(summed, "band", 0, 0, axis_index_groups=groups, tiled=True)
+    home = brought_home(partial.reshape(PW, PW * rows, width)).astype(BF16)
     screened = home.transpose(1, 0, 2).reshape(rows, 1, block)
 
-    spread = jnp.where(pick_jz[None], screened, jnp.zeros((), BF16)).reshape(rows * NJ * NK, block)
-    box = jnp.einsum("mg,kg->mk", spread, pick_x, preferred_element_type=F32)
-    mixed = dot("xk,mk->xm", jnp.concatenate([cos_k, sin_k], axis=0), box)
+    spread = (screened * pick_x[None]).reshape(rows * NK, block)
+    box = jnp.einsum("mg,kg->mk", pick_jz.astype(BF16), spread, preferred_element_type=F32)
+    box = box.reshape(NJ * NK, rows, NK)
+    mixed = dot("xk,mqk->xqm", jnp.concatenate([cos_k, sin_k], axis=0), box)
     mixed = mixed.reshape(2, GRID, pairs, 2, NJ * NK)
     real = mixed[0, :, :, 0] - mixed[1, :, :, 1]
     imag = mixed[0, :, :, 1] + mixed[1, :, :, 0]

time: 235 us -> 93.7 us (0.40)
  waiting for transfers between devices: 140 us -> 9.12 us
  Pallas kernels: 0 us -> 44.7 us
  blocking collectives: 26.3 us -> 0 us
  between operations: 13.7 us -> 0.32 us
  starting transfers between devices: 22.9 us -> 16.3 us
  local copies, waits for them, and re-layouts: 15.7 us -> 10.6 us
    all_gather x1 -> x0, waiting for transfers between devices: 127 us -> none  [body(): lax.all_gather(spectra.reshape(rows, block), 'band', axis=0, tiled=True)]
    pallas_call x0 -> x2, Pallas kernels: none -> 44.7 us  [the longest x1 25.6 us: gathered(): pl.pallas_call(gather_kernel, out_shape=jax.ShapeDtypeStruct((4, 8, 2, *o...]
    all_to_all x2 -> x0, blocking collectives: 26.3 us -> none  [the longest x1 13.9 us: body(): lax.all_to_all(partial.reshape(PW, PW * rows, width), 'pw', 0, 0, tiled=T...]
    ppermute x1 -> x0, starting transfers between devices: 4.9 us -> none  [body(): summed = lax.ppermute(summed, ('band', 'pw'), turn)]
    select_n x1 -> x0, local copies, waits for them, and re-layouts: 4.06 us -> none  [body(): jnp.where(pick_jz[None], screened, jnp.zeros((), BF16))]
    ppermute x1 -> x0, waiting for transfers between devices: 4.06 us -> none  [body(): summed = lax.ppermute(summed, ('band', 'pw'), turn)]
    dot_general x2, matrix products: 3.71 us -> 0.95 us  [the longest x1 0.48 us: body(): jnp.einsum('mg,kg->mk', pick_jz.astype(BF16), spread, preferred_element_t...]
  transfers between devices with their start and end apart: 4 -> 2, of which waited for: 4 -> 2; matrix products, arithmetic and copies ran while one was open for 1% -> 2% of each run, Pallas kernels for 0% -> 0%
where the time goes in v2:
time: 93.7 us; the launch traced here: 93.1 us
  Pallas kernels  44.7 us (48%)
  starting transfers between devices  16.3 us (17%)
  local copies, waits for them, and re-layouts  10.6 us (11%)
  waiting for transfers between devices  9.12 us (10%)
  matrix products  6.33 us (7%)
  other arithmetic  5.63 us (6%)
    pallas_call x1, Pallas kernels, gathered(): pl.pallas_call(gather_kernel, out_shape=jax.ShapeDtypeStruct((4, 8, 2, *o...  25.6 us
    pallas_call x1, Pallas kernels, brought_home(): pl.pallas_call(home_kernel, out_shape=jax.ShapeDtypeStruct((PW, rows, wid...  19.1 us
    all_to_all x1, starting transfers between devices, body(): pencil = lax.all_to_all(field, 'pw', 0, 0, tiled=True).reshape(GRID, -1)  10.1 us
    all_to_all x1, starting transfers between devices, body(): field = lax.all_to_all(pencil, 'pw', 0, 0, tiled=True)  6.25 us
    all_to_all x1, waiting for transfers between devices, body(): field = lax.all_to_all(pencil, 'pw', 0, 0, tiled=True)  5.25 us
    dot_general x6, matrix products, dot(): return jnp.einsum(spec, a, b, precision=PRECISE, preferred_element_type=F32)  4.29 us
    all_to_all x1, waiting for transfers between devices, body(): pencil = lax.all_to_all(field, 'pw', 0, 0, tiled=True).reshape(GRID, -1)  3.87 us
    mul x2, other arithmetic, body(): density = occupied.astype(F32) * virtual.astype(F32)  1.88 us
  transfers between devices with their start and end apart: 2, of which 2 were waited for; matrix products, arithmetic and copies ran while one was open for 2% of the time, Pallas kernels for 0%

profile of v2, /device:TPU:1, one launch (start us, length us, event | category | flops | bytes accessed | tf_op | source)
XLA Modules:
  0.0 93.1 jit_solution(8950409274224875776)
XLA Ops:
  0.0 0.2 fusion.76
  0.2 0.9 %bitcast_convert_fusion = f32[8,4096]{1,0:T(8,128)S(1)} fusion(bf16[1,8,4096]{2,1,0:T(8,128)(2,1)} %param.5), kind=kLoop, calls=%fused_computation.57 | loop fusion | flops 32768 | bytes 196608 | tf_op jit(solution)/shard_map/mul | solution.py:219
  1.1 0.9 %convert_multiply_fusion.1 = f32[2,8,4096]{2,1,0:T(8,128)S(1)} fusion(bf16[2,8,4096]{2,1,0:T(8,128)(2,1)} %param.4, f32[8,4096]{1,0:T(8,128)S(1)} %bitcast_convert_fusion), kind=kLoop, calls=%fused_computation.18 | loop fusion | flops 131072 | bytes 524288 | tf_op jit(solution)/shard_map/mul | solution.py:219
  2.1 0.2 reshape.233
  2.3 0.1 broadcast_add_fusion
  2.4 0.1 add.166
  2.5 0.2 fusion.79
  2.6 0.6 fusion.47
  3.2 1.1 %convolution_bitcast_fusion.1 = f32[2,8,80,66]{2,3,1,0:T(8,128)S(1)} fusion(f32[2,8,64,66]{3,2,1,0:T(8,128)S(1)} %fusion.47, f32[64,40]{0,1:T(8,128)S(1)} %get-tuple-element.24, f32[64,40]{0,1:T(8,128)S(1)} %get-tuple-element.23), kind=kOutput, calls=%fused_computation.7 | convolution fusion | flops 64885760 | bytes 628736 | tf_op jit(solution)/shard_map/pxyc,yk->pxkc/dot_general | solution.py:28
  4.3 0.3 copy.89
  4.6 0.8 reshape.234
  5.4 1.0 %fusion.98 = (f32[2,8,1,8,5,1,33]{6,5,4,3,2,1,0:T(1,128)S(1)}, f32[2,8,1,8,5,1,33]{6,5,4,3,2,1,0:T(1,128)S(1)}, f32[2,8,1,8,5,1,33]{6,5,4,3,2,1,0:T(1,128)S(1)}, f32[2,8,1,8,5,1,33]{6,5,4,3,2,1,0:T(1,128)S(1)}) fusion(f32[2,8,2,8,5,2,33]{6,5,4,3,2,1,0:T(2,128)S(1)} %reshape.234), kind=kLoop, calls=%fused_computation.152 | loop fusion | bytes 675840 | tf_op jit(solution)/shard_map/slice | solution.py:225
  6.4 0.1 fusion.21
  6.5 0.1 maximum_bitcast_fusion
  6.6 0.1 copy.94
  6.7 1.2 %reshape.235 = bf16[8,8,660]{2,1,0:T(8,128)(2,1)} reshape(bf16[8,8,2,2,5,33]{5,4,3,2,1,0:T(8,128)(2,1)S(1)} %copy.94) | data formatting | bytes 168960 | tf_op jit(solution)/shard_map/reshape | solution.py:228
  7.9 10.1 %all-to-all-start = ((bf16[8,8,660]{2,1,0:T(8,128)(2,1)}), bf16[8,8,660]{2,1,0:T(8,128)(2,1)S(1)}, u32[]{:S(2)}, u32[]{:S(2)}) async-start(bf16[8,8,660]{2,1,0:T(8,128)(2,1)} %reshape.235), calls=%async_computation | async-start | bytes 196608 | tf_op jit(solution)/shard_map/all_to_all | solution.py:229
  18.0 0.7 fusion.88
  18.8 0.7 fusion.83
  19.5 3.9 %all-to-all-done = bf16[8,8,660]{2,1,0:T(8,128)(2,1)S(1)} async-done(((bf16[8,8,660]{2,1,0:T(8,128)(2,1)}), bf16[8,8,660]{2,1,0:T(8,128)(2,1)S(1)}, u32[]{:S(2)}, u32[]{:S(2)}) %all-to-all-start) | async-done | bytes 84512 | tf_op jit(solution)/shard_map/all_to_all | solution.py:229
  23.4 0.1 dot_general.38
  23.5 0.3 fusion.26
  23.8 0.5 fusion.5
  24.3 0.6 convert_element_type.88.own_ref
  24.9 25.6 %shard_map.46 = bf16[4,8,2,4,2048]{4,3,2,1,0:T(4,128)(2,1)} custom-call(bf16[4,2048]{1,0:T(4,128)(2,1)} %convert_element_type.88.own_ref), custom_call_target="tpu_custom_call" | custom-call | tf_op jit(solution)/shard_map/pallas_call | solution.py:112
  50.5 1.3 %reshape.237 = bf16[256,2048]{1,0:T(8,128)(2,1)S(1)} reshape(bf16[4,8,2,4,2048]{4,3,2,1,0:T(4,128)(2,1)} %shard_map.46) | data formatting | bytes 2097152 | tf_op jit(solution)/shard_map/reshape | solution.py:240
  51.9 1.1 %convolution_convert_fusion = bf16[256,256]{1,0:T(8,128)(2,1)} fusion(bf16[256,2048]{1,0:T(8,128)(2,1)S(1)} %reshape.237, bf16[2048,256]{1,0:T(8,128)(2,1)S(1)} %copy-done), kind=kOutput, calls=%fused_computation.9 | convolution fusion | flops 268500992 | bytes 2228224 | tf_op jit(solution)/shard_map/dot_general | solution.py:241
  53.0 19.1 %shard_map.47 = f32[8,4,256]{2,1,0:T(4,128)} custom-call(bf16[8,32,256]{2,1,0:T(8,128)(2,1)} %bitcast.100), custom_call_target="tpu_custom_call" | custom-call | tf_op jit(solution)/shard_map/pallas_call | solution.py:184
  72.1 0.8 convert_element_type.90
  72.9 0.5 fusion.3
  73.4 0.8 convolution_bitcast_fusion.2
  74.1 0.2 copy.99
  74.4 0.1 copy.101
  74.5 0.8 convert_element_type.91
  75.3 6.3 %all-to-all-start.1 = ((bf16[8,8,660]{2,1,0:T(8,128)(2,1)}), bf16[8,8,660]{2,1,0:T(8,128)(2,1)S(1)}, u32[]{:S(2)}, u32[]{:S(2)}) async-start(bf16[8,8,660]{2,1,0:T(8,128)(2,1)} %convert_element_type.91), calls=%async_computation.1 | async-start | bytes 196608 | tf_op jit(solution)/shard_map/all_to_all | solution.py:255
  81.6 0.2 fusion.74
  81.7 5.2 %all-to-all-done.1 = bf16[8,8,660]{2,1,0:T(8,128)(2,1)S(1)} async-done(((bf16[8,8,660]{2,1,0:T(8,128)(2,1)}), bf16[8,8,660]{2,1,0:T(8,128)(2,1)S(1)}, u32[]{:S(2)}, u32[]{:S(2)}) %all-to-all-start.1) | async-done | bytes 84512 | tf_op jit(solution)/shard_map/all_to_all | solution.py:255
  87.0 0.9 reshape.240
  87.9 0.3 copy.102
  88.2 0.2 reshape.241
  88.4 0.5 convolution_bitcast_fusion
  88.9 0.6 reshape.255
  89.5 0.8 fusion.99
  90.3 0.4 copy.125
  90.7 0.4 copy.126
  91.1 1.1 %fusion.8 = f32[2,8,64,64]{3,2,1,0:T(8,128)S(1)} fusion(f32[2,8,64,66]{3,2,1,0:T(8,128)S(1)} %bitcast.97, f32[2,8,64,66]{3,2,1,0:T(8,128)S(1)} %bitcast.96, f32[33,64]{0,1:T(8,128)S(1)} %get-tuple-element.18, f32[33,64]{0,1:T(8,128)S(1)} %get-tuple-element.19, f32[33,64]{0,1:T(8,128)S(1)} %get-tuple-element.17), kind=kOutput, calls=%fused_computation.10 | convolution fusion | flops 103977984 | bytes 828160 | tf_op jit(solution)/shard_map/pxyc,cz->pxyz/dot_general | solution.py:28
  92.2 0.2 reshape.243
  92.4 0.7 fusion.20
  (14 shorter events, 0.1 us)
Async XLA Ops:
  0.0 51.9 %copy-start = (bf16[2048,256]{1,0:T(8,128)(2,1)S(1)}, bf16[2048,256]{1,0:T(8,128)(2,1)}, u32[]{:S(2)}) copy-start(bf16[2048,256]{1,0:T(8,128)(2,1)} %param.6) | copy-start | bytes 3145732
  7.9 15.5 %all-to-all-start = ((bf16[8,8,660]{2,1,0:T(8,128)(2,1)}), bf16[8,8,660]{2,1,0:T(8,128)(2,1)S(1)}, u32[]{:S(2)}, u32[]{:S(2)}) async-start(bf16[8,8,660]{2,1,0:T(8,128)(2,1)} %reshape.235), calls=%async_computation | async-start | bytes 196608 | tf_op jit(solution)/shard_map/all_to_all | solution.py:229
  75.3 11.7 %all-to-all-start.1 = ((bf16[8,8,660]{2,1,0:T(8,128)(2,1)}), bf16[8,8,660]{2,1,0:T(8,128)(2,1)S(1)}, u32[]{:S(2)}, u32[]{:S(2)}) async-start(bf16[8,8,660]{2,1,0:T(8,128)(2,1)} %convert_element_type.91), calls=%async_computation.1 | async-start | bytes 196608 | tf_op jit(solution)/shard_map/all_to_all | solution.py:255
  91.1 1.3 %copy-start.1 = (bf16[2,8,4096]{2,1,0:T(8,128)(2,1)S(1)}, bf16[2,8,4096]{2,1,0:T(8,128)(2,1)}, u32[]{:S(2)}) copy-start(bf16[2,8,4096]{2,1,0:T(8,128)(2,1)} %param.4) | copy-start | bytes 393220

commit v3 on v2

--- a/solution.py
+++ b/solution.py
@@ -37,17 +37,13 @@
     )
 
 
-def greet(devices, count):
-    barrier = pltpu.get_barrier_semaphore()
-    for device in devices:
-        pl.semaphore_signal(barrier, inc=1, device_id=device, device_id_type=MESH)
-    pl.semaphore_wait(barrier, count)
-
-
 OFFSETS = (1, 7, 2, 6, 3, 5, 4)
 
 
-def gather_kernel(own_ref, all_ref, own_sem, z_sems, ys_sems, yr_sems, xs_sems, xr_sems, fs_sems, fr_sems):
+def screen_kernel(
+    own_ref, screening_ref, home_ref, all_ref, part_ref, landed, summed, own_sem, z_sems, ys_sems,
+    yr_sems, xs_sems, xr_sems, fs_sems, fr_sems, ps_sems, pr_sems, cs_sems, cr_sems
+):
     band, pw = lax.axis_index("band"), lax.axis_index("pw")
     x, y, z = band // 16, lax.rem(band // 2, 8), lax.rem(band, 2)
 
@@ -60,7 +56,21 @@
     right, left = lax.rem(x + 1, 4), lax.rem(x + 3, 4)
     across = at(x, y, 1 - z)
     beside = (at(right, y, z), at(left, y, z))
-    greet([across, *beside, *[at(x, up(d), z) for d in OFFSETS]], 3 + len(OFFSETS))
+    high, low = band // PW, lax.rem(band, PW)
+    same = high == pw
+
+    def over(d):
+        return lax.rem(pw + d, PW)
+
+    barrier = pltpu.get_barrier_semaphore()
+    for t in range(PW):
+        @pl.when(jnp.logical_not(same & (low == t)))
+        def _():
+            pl.semaphore_signal(barrier, inc=1, device_id=(pw * PW + t, high), device_id_type=MESH)
+    near = [across, *beside, *[at(x, up(d), z) for d in OFFSETS], *[(band, over(d)) for d in range(1, PW)]]
+    for device in near:
+        pl.semaphore_signal(barrier, inc=1, device_id=device, device_id_type=MESH)
+    pl.semaphore_wait(barrier, len(near) + PW - jnp.where(same, 1, 0))
 
     keep = pltpu.make_async_copy(own_ref, all_ref.at[x, y, z], own_sem)
     keep.start()
@@ -102,41 +112,10 @@
                 forwards.append(copy)
     for copy in forwards:
         copy.wait_recv()
-    to_across.wait_send()
-    for copy in [*y_copies.values(), *x_copies, *forwards]:
-        copy.wait_send()
-
-
-def gathered(own):
-    dma = pltpu.SemaphoreType.DMA
-    return pl.pallas_call(
-        gather_kernel,
-        out_shape=jax.ShapeDtypeStruct((4, 8, 2, *own.shape), own.dtype),
-        in_specs=[pl.BlockSpec(memory_space=pltpu.VMEM)],
-        out_specs=pl.BlockSpec(memory_space=pltpu.VMEM),
-        scratch_shapes=[
-            dma, dma((2,)), dma((2, 8)), dma((2, 8)), dma((2, 8)), dma((2, 8)), dma((8,)), dma((8,))
-        ],
-        compiler_params=pltpu.CompilerParams(collective_id=0, has_side_effects=True),
-    )(own)
-
-
-def home_kernel(part_ref, home_ref, landed, summed, ps_sems, pr_sems, cs_sems, cr_sems, own_sem):
-    band, pw = lax.axis_index("band"), lax.axis_index("pw")
-    high, low = band // PW, lax.rem(band, PW)
-    same = high == pw
-
-    def over(d):
-        return lax.rem(pw + d, PW)
-
-    barrier = pltpu.get_barrier_semaphore()
-    for d in range(1, PW):
-        pl.semaphore_signal(barrier, inc=1, device_id=(band, over(d)), device_id_type=MESH)
-    for t in range(PW):
-        @pl.when(jnp.logical_not(same & (low == t)))
-        def _():
-            pl.semaphore_signal(barrier, inc=1, device_id=(pw * PW + t, high), device_id_type=MESH)
-    pl.semaphore_wait(barrier, jnp.where(same, 2 * PW - 2, 2 * PW - 1))
+    rows = all_ref.shape[3]
+    everyone = all_ref[...].reshape(BAND * rows, all_ref.shape[4])
+    partial = jnp.dot(everyone, screening_ref[...], preferred_element_type=F32).astype(BF16)
+    part_ref[...] = partial.reshape(part_ref.shape)
 
     copies = []
     for d in range(1, PW):
@@ -147,11 +126,10 @@
     for d in range(1, PW):
         copies[d - 1].wait_recv()
         total = total + landed[lax.rem(pw + PW - d, PW)].astype(F32)
-    rows = total.shape[0] // PW
     for t in range(PW):
         summed[t] = total[t * rows : (t + 1) * rows]
 
-    def across(t, sem):
+    def send_home(t, sem):
         return remote(summed.at[t], home_ref.at[low], cs_sems.at[t], cr_sems.at[sem], (pw * PW + t, high))
 
     for t in range(PW):
@@ -165,7 +143,7 @@
 
         @pl.when(jnp.logical_not(mine))
         def _():
-            across(t, low).start()
+            send_home(t, low).start()
 
     for t in range(PW):
         @pl.when(jnp.logical_not(same & (low == t)))
@@ -176,22 +154,29 @@
             ).wait()
     for copy in copies:
         copy.wait_send()
-
-
-def brought_home(partial):
+    to_across.wait_send()
+    for copy in [*y_copies.values(), *x_copies, *forwards]:
+        copy.wait_send()
+
+
+def screened_home(own, screening):
     dma = pltpu.SemaphoreType.DMA
-    rows, width = partial.shape[1] // PW, partial.shape[2]
+    rows, width = own.shape[0], screening.shape[1]
     return pl.pallas_call(
-        home_kernel,
+        screen_kernel,
         out_shape=jax.ShapeDtypeStruct((PW, rows, width), F32),
-        in_specs=[pl.BlockSpec(memory_space=pltpu.VMEM)],
+        in_specs=[pl.BlockSpec(memory_space=pltpu.VMEM)] * 2,
         out_specs=pl.BlockSpec(memory_space=pltpu.VMEM),
         scratch_shapes=[
-            pltpu.VMEM(partial.shape, BF16), pltpu.VMEM((PW, rows, width), F32),
-            dma((PW,)), dma((PW,)), dma((PW,)), dma((PW,)), dma,
+            pltpu.VMEM((4, 8, 2, *own.shape), BF16),
+            pltpu.VMEM((PW, PW * rows, width), BF16),
+            pltpu.VMEM((PW, PW * rows, width), BF16),
+            pltpu.VMEM((PW, rows, width), F32),
+            dma, dma((2,)), dma((2, 8)), dma((2, 8)), dma((2, 8)), dma((2, 8)), dma((8,)), dma((8,)),
+            dma((PW,)), dma((PW,)), dma((PW,)), dma((PW,)),
         ],
-        compiler_params=pltpu.CompilerParams(collective_id=1, has_side_effects=True),
-    )(partial)
+        compiler_params=pltpu.CompilerParams(collective_id=0, has_side_effects=True),
+    )(own, screening)
 
 
 def body(occupied, virtual, screening, grid_index):
@@ -237,11 +222,7 @@
     spectra = jnp.sum(columns * pick_x.astype(F32), axis=2).astype(BF16)
 
     rows = pairs * 2
-    everyone = gathered(spectra.reshape(rows, block)).reshape(BAND * rows, block)
-    partial = jnp.dot(everyone, screening, preferred_element_type=F32).astype(BF16)
-
-    width = screening.shape[1]
-    home = brought_home(partial.reshape(PW, PW * rows, width)).astype(BF16)
+    home = screened_home(spectra.reshape(rows, block), screening).astype(BF16)
     screened = home.transpose(1, 0, 2).reshape(rows, 1, block)
 
     spread = (screened * pick_x[None]).reshape(rows * NK, block)

time: 93.7 us -> 86.2 us (0.920)
  Pallas kernels: 44.7 us -> 42.1 us
  starting transfers between devices: 16.3 us -> 14.1 us
  local copies, waits for them, and re-layouts: 10.6 us -> 9.28 us
  matrix products: 6.33 us -> 5.24 us
    pallas_call x2 -> x1, Pallas kernels: 44.7 us -> 42.1 us  [screened_home(): pl.pallas_call(screen_kernel, out_shape=jax.ShapeDtypeStruct((PW, rows, w...]
    all_to_all x1, starting transfers between devices: 6.25 us -> 4 us  [body(): field = lax.all_to_all(pencil, 'pw', 0, 0, tiled=True)]
    reshape x1 -> x0, local copies, waits for them, and re-layouts: 1.34 us -> none  [body(): gathered(spectra.reshape(rows, block)).reshape(BAND * rows, block)]
    dot_general x1 -> x0, matrix products: 1.1 us -> none  [body(): jnp.dot(everyone, screening, preferred_element_type=F32).astype(BF16)]
where the time goes in v3:
time: 86.2 us; the launch traced here: 85.6 us
  Pallas kernels  42.1 us (49%)
  starting transfers between devices  14.1 us (16%)
  local copies, waits for them, and re-layouts  9.28 us (11%)
  waiting for transfers between devices  9.08 us (11%)
  other arithmetic  5.54 us (6%)
  matrix products  5.24 us (6%)
    pallas_call x1, Pallas kernels, screened_home(): pl.pallas_call(screen_kernel, out_shape=jax.ShapeDtypeStruct((PW, rows, w...  42.1 us
    all_to_all x1, starting transfers between devices, body(): pencil = lax.all_to_all(field, 'pw', 0, 0, tiled=True).reshape(GRID, -1)  10.1 us
    all_to_all x1, waiting for transfers between devices, body(): field = lax.all_to_all(pencil, 'pw', 0, 0, tiled=True)  5.21 us
    dot_general x6, matrix products, dot(): return jnp.einsum(spec, a, b, precision=PRECISE, preferred_element_type=F32)  4.29 us
    all_to_all x1, starting transfers between devices, body(): field = lax.all_to_all(pencil, 'pw', 0, 0, tiled=True)  4 us
    all_to_all x1, waiting for transfers between devices, body(): pencil = lax.all_to_all(field, 'pw', 0, 0, tiled=True).reshape(GRID, -1)  3.87 us
    mul x2, other arithmetic, body(): density = occupied.astype(F32) * virtual.astype(F32)  1.79 us
  transfers between devices with their start and end apart: 2, of which 2 were waited for; matrix products, arithmetic and copies ran while one was open for 2% of the time, Pallas kernels for 0%

profile of v3, /device:TPU:1, one launch (start us, length us, event | category | flops | bytes accessed | tf_op | source)
XLA Modules:
  0.0 85.6 jit_solution(935304092629170835)
XLA Ops:
  0.0 0.2 fusion.76
  0.2 0.9 bitcast_convert_fusion
  1.0 0.9 %convert_multiply_fusion.1 = f32[2,8,4096]{2,1,0:T(8,128)S(1)} fusion(bf16[2,8,4096]{2,1,0:T(8,128)(2,1)} %param.4, f32[8,4096]{1,0:T(8,128)S(1)} %bitcast_convert_fusion), kind=kLoop, calls=%fused_computation.17 | loop fusion | flops 131072 | bytes 524288 | tf_op jit(solution)/shard_map/mul | solution.py:204
  2.0 0.2 reshape.227
  2.2 0.1 broadcast_add_fusion
  2.3 0.1 add.166
  2.4 0.2 fusion.79
  2.5 0.6 fusion.47
  3.1 1.1 %convolution_bitcast_fusion.1 = f32[2,8,80,66]{2,3,1,0:T(8,128)S(1)} fusion(f32[2,8,64,66]{3,2,1,0:T(8,128)S(1)} %fusion.47, f32[64,40]{0,1:T(8,128)S(1)} %get-tuple-element.24, f32[64,40]{0,1:T(8,128)S(1)} %get-tuple-element.23), kind=kOutput, calls=%fused_computation.7 | convolution fusion | flops 64885760 | bytes 628736 | tf_op jit(solution)/shard_map/pxyc,yk->pxkc/dot_general | solution.py:28
  4.2 0.3 copy.89
  4.5 0.8 reshape.228
  5.3 1.0 %fusion.98 = (f32[2,8,1,8,5,1,33]{6,5,4,3,2,1,0:T(1,128)S(1)}, f32[2,8,1,8,5,1,33]{6,5,4,3,2,1,0:T(1,128)S(1)}, f32[2,8,1,8,5,1,33]{6,5,4,3,2,1,0:T(1,128)S(1)}, f32[2,8,1,8,5,1,33]{6,5,4,3,2,1,0:T(1,128)S(1)}) fusion(f32[2,8,2,8,5,2,33]{6,5,4,3,2,1,0:T(2,128)S(1)} %reshape.228), kind=kLoop, calls=%fused_computation.151 | loop fusion | bytes 675840 | tf_op jit(solution)/shard_map/slice | solution.py:210
  6.3 0.1 fusion.21
  6.4 0.1 maximum_bitcast_fusion
  6.5 0.1 copy.94
  6.6 1.2 %reshape.229 = bf16[8,8,660]{2,1,0:T(8,128)(2,1)} reshape(bf16[8,8,2,2,5,33]{5,4,3,2,1,0:T(8,128)(2,1)S(1)} %copy.94) | data formatting | bytes 168960 | tf_op jit(solution)/shard_map/reshape | solution.py:213
  7.8 10.1 %all-to-all-start = ((bf16[8,8,660]{2,1,0:T(8,128)(2,1)}), bf16[8,8,660]{2,1,0:T(8,128)(2,1)S(1)}, u32[]{:S(2)}, u32[]{:S(2)}) async-start(bf16[8,8,660]{2,1,0:T(8,128)(2,1)} %reshape.229), calls=%async_computation | async-start | bytes 196608 | tf_op jit(solution)/shard_map/all_to_all | solution.py:214
  17.9 0.7 fusion.88
  18.7 0.7 fusion.83
  19.4 3.9 %all-to-all-done = bf16[8,8,660]{2,1,0:T(8,128)(2,1)S(1)} async-done(((bf16[8,8,660]{2,1,0:T(8,128)(2,1)}), bf16[8,8,660]{2,1,0:T(8,128)(2,1)S(1)}, u32[]{:S(2)}, u32[]{:S(2)}) %all-to-all-start) | async-done | bytes 84512 | tf_op jit(solution)/shard_map/all_to_all | solution.py:214
  23.3 0.1 dot_general.35
  23.4 0.3 fusion.26
  23.7 0.5 fusion.5
  24.2 0.6 convert_element_type.85.own_ref
  24.8 42.1 %shard_map.46 = f32[8,4,256]{2,1,0:T(4,128)} custom-call(bf16[4,2048]{1,0:T(4,128)(2,1)} %convert_element_type.85.own_ref, bf16[2048,256]{1,0:T(8,128)(2,1)} %screening_ref.1), custom_call_target="tpu_custom_call" | custom-call | tf_op jit(solution)/shard_map/pallas_call | solution.py:165
  66.9 0.8 convert_element_type.86
  67.7 0.5 fusion.3
  68.2 0.8 convolution_bitcast_fusion.2
  68.9 0.2 copy.99
  69.2 0.1 copy.101
  69.3 0.8 convert_element_type.87
  70.1 4.0 %all-to-all-start.1 = ((bf16[8,8,660]{2,1,0:T(8,128)(2,1)}), bf16[8,8,660]{2,1,0:T(8,128)(2,1)S(1)}, u32[]{:S(2)}, u32[]{:S(2)}) async-start(bf16[8,8,660]{2,1,0:T(8,128)(2,1)} %convert_element_type.87), calls=%async_computation.1 | async-start | bytes 196608 | tf_op jit(solution)/shard_map/all_to_all | solution.py:236
  74.1 0.2 fusion.74
  74.3 5.2 %all-to-all-done.1 = bf16[8,8,660]{2,1,0:T(8,128)(2,1)S(1)} async-done(((bf16[8,8,660]{2,1,0:T(8,128)(2,1)}), bf16[8,8,660]{2,1,0:T(8,128)(2,1)S(1)}, u32[]{:S(2)}, u32[]{:S(2)}) %all-to-all-start.1) | async-done | bytes 84512 | tf_op jit(solution)/shard_map/all_to_all | solution.py:236
  79.5 0.9 %reshape.232 = bf16[8,8,2,2,5,33]{5,4,3,2,1,0:T(8,128)(2,1)S(1)} reshape(bf16[8,8,660]{2,1,0:T(8,128)(2,1)S(1)} %all-to-all-done.1) | data formatting | bytes 168960 | tf_op jit(solution)/shard_map/reshape | solution.py:237
  80.4 0.3 copy.102
  80.7 0.2 reshape.233
  80.9 0.5 convolution_bitcast_fusion
  81.4 0.6 reshape.247
  82.0 0.8 fusion.99
  82.8 0.4 copy.125
  83.2 0.4 copy.126
  83.6 0.0 copy-start
  83.6 1.1 %fusion.8 = f32[2,8,64,64]{3,2,1,0:T(8,128)S(1)} fusion(f32[2,8,64,66]{3,2,1,0:T(8,128)S(1)} %bitcast.94, f32[2,8,64,66]{3,2,1,0:T(8,128)S(1)} %bitcast.93, f32[33,64]{0,1:T(8,128)S(1)} %get-tuple-element.18, f32[33,64]{0,1:T(8,128)S(1)} %get-tuple-element.19, f32[33,64]{0,1:T(8,128)S(1)} %get-tuple-element.17), kind=kOutput, calls=%fused_computation.9 | convolution fusion | flops 103977984 | bytes 828160 | tf_op jit(solution)/shard_map/pxyc,cz->pxyz/dot_general | solution.py:28
  84.7 0.2 reshape.235
  84.9 0.0 copy-done
  84.9 0.7 fusion.20
  (10 shorter events, 0.1 us)
Async XLA Ops:
  7.8 15.5 %all-to-all-start = ((bf16[8,8,660]{2,1,0:T(8,128)(2,1)}), bf16[8,8,660]{2,1,0:T(8,128)(2,1)S(1)}, u32[]{:S(2)}, u32[]{:S(2)}) async-start(bf16[8,8,660]{2,1,0:T(8,128)(2,1)} %reshape.229), calls=%async_computation | async-start | bytes 196608 | tf_op jit(solution)/shard_map/all_to_all | solution.py:214
  70.1 9.4 %all-to-all-start.1 = ((bf16[8,8,660]{2,1,0:T(8,128)(2,1)}), bf16[8,8,660]{2,1,0:T(8,128)(2,1)S(1)}, u32[]{:S(2)}, u32[]{:S(2)}) async-start(bf16[8,8,660]{2,1,0:T(8,128)(2,1)} %convert_element_type.87), calls=%async_computation.1 | async-start | bytes 196608 | tf_op jit(solution)/shard_map/all_to_all | solution.py:236
  83.6 1.3 %copy-start = (bf16[2,8,4096]{2,1,0:T(8,128)(2,1)S(1)}, bf16[2,8,4096]{2,1,0:T(8,128)(2,1)}, u32[]{:S(2)}) copy-start(bf16[2,8,4096]{2,1,0:T(8,128)(2,1)} %param.4) | copy-start | bytes 393220

commit v4 on v3

--- a/solution.py
+++ b/solution.py
@@ -179,6 +179,40 @@
     )(own, screening)
 
 
+def exchange_kernel(from_ref, to_ref, own_sem, s_sems, r_sems):
+    band, pw = lax.axis_index("band"), lax.axis_index("pw")
+
+    def over(d):
+        return lax.rem(pw + d, PW)
+
+    barrier = pltpu.get_barrier_semaphore()
+    for d in range(1, PW):
+        pl.semaphore_signal(barrier, inc=1, device_id=(band, over(d)), device_id_type=MESH)
+    own = pltpu.make_async_copy(from_ref.at[pw], to_ref.at[pw], own_sem)
+    own.start()
+    pl.semaphore_wait(barrier, PW - 1)
+    copies = []
+    for d in range(1, PW):
+        copy = remote(from_ref.at[over(d)], to_ref.at[pw], s_sems.at[d], r_sems.at[d], (band, over(d)))
+        copy.start()
+        copies.append(copy)
+    own.wait()
+    for copy in copies:
+        copy.wait()
+
+
+def exchanged(blocks, collective_id):
+    dma = pltpu.SemaphoreType.DMA
+    return pl.pallas_call(
+        exchange_kernel,
+        out_shape=jax.ShapeDtypeStruct(blocks.shape, blocks.dtype),
+        in_specs=[pl.BlockSpec(memory_space=pltpu.VMEM)],
+        out_specs=pl.BlockSpec(memory_space=pltpu.VMEM),
+        scratch_shapes=[dma, dma((PW,)), dma((PW,))],
+        compiler_params=pltpu.CompilerParams(collective_id=collective_id, has_side_effects=True),
+    )(blocks)
+
+
 def body(occupied, virtual, screening, grid_index):
     pairs, planes = occupied.shape[0], occupied.shape[1]
     slab = lax.axis_index("pw")
@@ -201,17 +235,20 @@
     pick_x = (jnp.arange(NK, dtype=jnp.int32)[:, None] == at_x[None]).astype(BF16)
     pick_jz = jnp.arange(NJ * NK, dtype=jnp.int32)[:, None] == at_jz[None]
 
-    density = occupied.astype(F32) * virtual.astype(F32)
-    density = density.reshape(pairs, planes, GRID, GRID)
-    forward_z = jnp.concatenate([cos_k, -sin_k], axis=1)
-    field = dot("pxyz,zc->pxyc", density, forward_z)
-    both_y = jnp.concatenate([cos_y, sin_y], axis=1)
-    mixed = dot("pxyc,yk->pxkc", field, both_y).reshape(pairs, planes, 2, PW, NJ, 2, NK)
-    real = mixed[:, :, 0, :, :, 0] + mixed[:, :, 1, :, :, 1]
-    imag = mixed[:, :, 0, :, :, 1] - mixed[:, :, 1, :, :, 0]
-    field = jnp.stack([real, imag], axis=0).astype(BF16)
-    field = field.transpose(3, 2, 1, 0, 4, 5).reshape(PW, planes, pairs * 2 * NJ * NK)
-    pencil = lax.all_to_all(field, "pw", 0, 0, tiled=True).reshape(GRID, -1)
+    c = cos_y.reshape(GRID, PW, 1, NJ)
+    n = sin_y.reshape(GRID, PW, 1, NJ)
+    to_rows = jnp.concatenate(
+        [jnp.concatenate([c, -n], axis=2), jnp.concatenate([n, c], axis=2)], axis=0
+    ).reshape(2 * GRID, PW * 2 * NJ)
+
+    occ = occupied.reshape(pairs, planes, GRID, GRID).astype(F32)
+    density = occ * virtual.reshape(1, planes, GRID, GRID).astype(F32)
+    field = jnp.concatenate(
+        [dot("pxyz,zc->pxyc", density, cos_k), dot("pxyz,zc->pxyc", density, -sin_k)], axis=2
+    )
+    field = dot("yk,pxyc->pxkc", to_rows, field).astype(BF16)
+    field = field.reshape(pairs, planes, PW, 2 * NJ, NK).transpose(2, 1, 0, 3, 4)
+    pencil = exchanged(field.reshape(PW, planes, pairs * 2 * NJ * NK), 1).reshape(GRID, -1)
 
     cos_sin = jnp.concatenate([cos_k, sin_k], axis=1)
     mixed = dot("xm,xk->mk", pencil.astype(F32), cos_sin).reshape(pairs, 2, NJ * NK, 2, NK)
@@ -233,17 +270,13 @@
     real = mixed[0, :, :, 0] - mixed[1, :, :, 1]
     imag = mixed[0, :, :, 1] + mixed[1, :, :, 0]
     pencil = jnp.stack([real, imag], axis=2).astype(BF16).reshape(PW, planes, -1)
-    field = lax.all_to_all(pencil, "pw", 0, 0, tiled=True)
-    field = field.reshape(PW, planes, pairs, 2, NJ, NK).astype(F32)
-    field = field.transpose(2, 1, 0, 4, 3, 5).reshape(pairs, planes, PW * NJ, 2 * NK)
-    mixed = dot("pxkc,yk->pxyc", field, jnp.concatenate([cos_y, sin_y], axis=0))
-    mixed = mixed.reshape(pairs, planes, 2, GRID, 2 * NK)
-    mixed = jnp.concatenate([mixed[:, :, 0], mixed[:, :, 1]], axis=-1)
-    cz, sz = jnp.transpose(cos_k), jnp.transpose(sin_k)
-    back = jnp.concatenate([cz, -sz, -sz, -cz], axis=0) * (1.0 / math.sqrt(NG))
-    potential = dot("pxyc,cz->pxyz", mixed, back)
-    weighted = potential.reshape(pairs, planes, GRID * GRID) * occupied.astype(F32)
-    return jnp.sum(weighted, axis=0)[None]
+    field = exchanged(pencil, 2).reshape(PW, planes, pairs, 2 * NJ, NK)
+    field = field.transpose(2, 1, 0, 3, 4).reshape(pairs, planes, PW * 2 * NJ, NK).astype(F32)
+    mixed = dot("yk,pxkc->pxyc", to_rows, field)
+    norm_out = 1.0 / math.sqrt(NG)
+    potential = dot("pxyc,zc->pxyz", mixed[:, :, :GRID], cos_k * norm_out)
+    potential = potential - dot("pxyc,zc->pxyz", mixed[:, :, GRID:], sin_k * norm_out)
+    return jnp.sum(potential * occ, axis=0).reshape(1, planes, GRID * GRID)
 
 
 def solution(mesh):

time: 86.2 us -> 85.9 us (level)
  Pallas kernels: 42.1 us -> 64.7 us
  starting transfers between devices: 14.1 us -> 0 us
  waiting for transfers between devices: 9.08 us -> 0 us
  matrix products: 5.24 us -> 8.4 us
  other arithmetic: 5.54 us -> 2.89 us
    pallas_call x0 -> x2, Pallas kernels: none -> 22.3 us  [exchanged(): pl.pallas_call(exchange_kernel, out_shape=jax.ShapeDtypeStruct(blocks.sha...]
    all_to_all x2 -> x0, starting transfers between devices: 14.1 us -> none  [the longest x1 10.1 us: body(): pencil = lax.all_to_all(field, 'pw', 0, 0, tiled=True).reshape(GRID, -1)]
    all_to_all x2 -> x0, waiting for transfers between devices: 9.08 us -> none  [the longest x1 5.21 us: body(): field = lax.all_to_all(pencil, 'pw', 0, 0, tiled=True)]
    dot_general x6 -> x8, matrix products: 4.29 us -> 7.46 us  [dot(): return jnp.einsum(spec, a, b, precision=PRECISE, preferred_element_type=F32)]
    convert_element_type x0 -> x3, local copies, waits for them, and re-layouts: none -> 2.38 us  [the longest x1 1.11 us: body(): occ = occupied.reshape(pairs, planes, GRID, GRID).astype(F32)]
    slice x2 -> x0, local copies, waits for them, and re-layouts: 1.85 us -> none  [the longest x1 1.01 us: body(): real = mixed[:, :, 0, :, :, 0] + mixed[:, :, 1, :, :, 1]]
    mul x2 -> x0, other arithmetic: 1.79 us -> none  [body(): density = occupied.astype(F32) * virtual.astype(F32)]
    dot_general x2, local copies, waits for them, and re-layouts: 0.15 us -> 1.04 us  [dot(): return jnp.einsum(spec, a, b, precision=PRECISE, preferred_element_type=F32)]
  transfers between devices with their start and end apart: 2 -> 0, of which waited for: 2 -> 0; matrix products, arithmetic and copies ran while one was open for 2% -> 0% of each run, Pallas kernels for 0% -> 0%
where the time goes in v4:
time: 85.9 us; the launch traced here: 85.4 us
  Pallas kernels  64.7 us (75%)
  local copies, waits for them, and re-layouts  9.21 us (11%)
  matrix products  8.4 us (10%)
  other arithmetic  2.89 us (3%)
    pallas_call x1, Pallas kernels, screened_home(): pl.pallas_call(screen_kernel, out_shape=jax.ShapeDtypeStruct((PW, rows, w...  42.3 us
    pallas_call x2, Pallas kernels, exchanged(): pl.pallas_call(exchange_kernel, out_shape=jax.ShapeDtypeStruct(blocks.sha...  22.3 us
    dot_general x8, matrix products, dot(): return jnp.einsum(spec, a, b, precision=PRECISE, preferred_element_type=F32)  7.46 us
    reshape x1, local copies, waits for them, and re-layouts, body(): field = exchanged(pencil, 2).reshape(PW, planes, pairs, 2 * NJ, NK)  1.81 us

profile of v4, /device:TPU:1, one launch (start us, length us, event | category | flops | bytes accessed | tf_op | source)
XLA Modules:
  0.0 85.4 jit_solution(1998998571864370486)
XLA Ops:
  0.0 1.1 %reshape.291 = f32[2,8,64,64]{3,2,1,0:T(8,128)S(1)} reshape(bf16[2,8,4096]{2,1,0:T(8,128)(2,1)} %param.4) | data formatting | bytes 393216 | tf_op jit(solution)/shard_map/convert_element_type | solution.py:244
  1.1 1.0 %reshape.292 = f32[8,64,64]{2,1,0:T(8,128)S(1)} reshape(bf16[1,8,4096]{2,1,0:T(8,128)(2,1)} %param.5) | data formatting | bytes 196608 | tf_op jit(solution)/shard_map/convert_element_type | solution.py:245
  2.1 1.7 %fusion.14 = f32[2,8,64,33]{2,3,1,0:T(8,128)S(1)} fusion(f32[2,8,64,64]{3,2,1,0:T(8,128)S(1)} %reshape.291, f32[8,64,64]{2,1,0:T(8,128)S(1)} %reshape.292, s32[33]{0:T(128)S(1)} %iota_add_fusion.1), kind=kOutput, calls=%fused_computation.16 | convolution fusion | flops 26049472 | bytes 528516 | tf_op jit(solution)/shard_map/pxyz,zc->pxyc/dot_general | solution.py:28
  3.8 1.7 %fusion.16 = f32[2,8,64,33]{2,3,1,0:T(8,128)S(1)} fusion(f32[2,8,64,64]{3,2,1,0:T(8,128)S(1)} %reshape.291, f32[8,64,64]{2,1,0:T(8,128)S(1)} %reshape.292, s32[33]{0:T(128)S(1)} %iota_add_fusion.1), kind=kOutput, calls=%fused_computation.18 | convolution fusion | flops 26047360 | bytes 528516 | tf_op jit(solution)/shard_map/pxyz,zc->pxyc/dot_general | solution.py:28
  5.5 0.1 broadcast_add_fusion
  5.6 0.2 fusion.68
  5.8 0.1 maximum_maximum_fusion
  5.9 0.5 fusion.10
  6.4 0.3 copy.14
  6.7 0.1 copy.15
  6.8 1.3 %reshape.285.from_ref = bf16[8,8,660]{2,1,0:T(8,128)(2,1)} reshape(bf16[8,8,2,10,33]{4,3,2,1,0:T(8,128)(2,1)S(1)} %copy.15) | data formatting | bytes 168960 | tf_op jit(solution)/shard_map/reshape | solution.py:251
  8.0 14.4 %shard_map.46 = bf16[8,8,660]{2,1,0:T(8,128)(2,1)} custom-call(bf16[8,8,660]{2,1,0:T(8,128)(2,1)} %reshape.285.from_ref), custom_call_target="tpu_custom_call" | custom-call | tf_op jit(solution)/shard_map/pallas_call | solution.py:206
  22.4 1.0 %dot_general.42 = bf16[2,2,165,64]{2,1,0,3:T(2,128)(2,1)S(1)} reshape(bf16[660,64]{0,1:T(8,128)(2,1)} %bitcast.90) | data formatting | bytes 168960 | tf_op jit(solution)/shard_map/xm,xk->mk/dot_general | solution.py:28
  23.5 0.2 fusion.72
  23.7 0.3 fusion.33
  24.0 0.7 fusion.85
  24.7 0.7 fusion.80
  25.5 0.5 fusion.5
  26.0 0.6 convert_element_type.117.own_ref
  26.6 42.3 %shard_map.47 = f32[8,4,256]{2,1,0:T(4,128)} custom-call(bf16[4,2048]{1,0:T(4,128)(2,1)} %convert_element_type.117.own_ref, bf16[2048,256]{1,0:T(8,128)(2,1)} %screening_ref.1), custom_call_target="tpu_custom_call" | custom-call | tf_op jit(solution)/shard_map/pallas_call | solution.py:165
  68.9 0.8 convert_element_type.118
  69.7 0.5 fusion.3
  70.2 0.8 convolution_bitcast_fusion
  70.9 0.2 copy.20
  71.2 0.1 copy.21
  71.4 0.8 convert_element_type.119.from_ref
  72.1 7.9 %shard_map.48 = bf16[8,8,660]{2,1,0:T(8,128)(2,1)} custom-call(bf16[8,8,660]{2,1,0:T(8,128)(2,1)} %convert_element_type.119.from_ref), custom_call_target="tpu_custom_call" | custom-call | tf_op jit(solution)/shard_map/pallas_call | solution.py:206
  80.0 1.8 %reshape.288 = bf16[8,8,2,10,33]{4,3,2,1,0:T(8,128)(2,1)S(1)} reshape(bf16[8,8,660]{2,1,0:T(8,128)(2,1)} %shard_map.48) | data formatting | bytes 168960 | tf_op jit(solution)/shard_map/reshape | solution.py:273
  81.9 0.1 copy.22
  82.0 0.4 convolution_bitcast_fusion.1
  82.4 1.0 %fusion.19 = f32[2,8,64,64]{3,2,1,0:T(8,128)S(1)} fusion(f32[2,8,128,33]{2,3,1,0:T(8,128)S(1)} %convolution_bitcast_fusion.1, s32[33]{0:T(128)S(1)} %iota_add_fusion.1), kind=kOutput, calls=%fused_computation.21 | convolution fusion | flops 25983936 | bytes 532612 | tf_op jit(solution)/shard_map/pxyc,zc->pxyz/dot_general | solution.py:28
  83.5 1.2 %fusion.9 = f32[8,64,64]{2,1,0:T(8,128)S(1)} fusion(f32[2,8,64,64]{3,2,1,0:T(8,128)S(1)} %reshape.291, f32[2,8,64,64]{3,2,1,0:T(8,128)S(1)} %fusion.19, f32[2,8,128,33]{2,3,1,0:T(8,128)S(1)} %convolution_bitcast_fusion.1, s32[33]{0:T(128)S(1)} %iota_add_fusion.1), kind=kOutput, calls=%fused_computation.8 | convolution fusion | flops 26147776 | bytes 925828 | tf_op jit(solution)/shard_map/pxyc,zc->pxyz/dot_general | solution.py:28
  84.6 0.8 reshape.290
  (11 shorter events, 0.1 us)

commit v5 on v4

--- a/solution.py
+++ b/solution.py
@@ -76,42 +76,55 @@
     keep.start()
     to_across = remote(own_ref, all_ref.at[x, y, z], z_sems.at[0], z_sems.at[1], across)
     to_across.start()
-    y_copies = {}
-    for d in OFFSETS:
-        y_copies[0, d] = remote(
-            own_ref, all_ref.at[x, y, z], ys_sems.at[0, d], yr_sems.at[0, d], at(x, up(d), z)
-        )
-        y_copies[0, d].start()
+    order = (0,) + OFFSETS
+    layers = (z, 1 - z)
+    y_copies, x_copies, forwards = {}, {}, {}
+
+    def along_y(h, source):
+        for d in OFFSETS:
+            copy = remote(
+                source, all_ref.at[x, y, layers[h]], ys_sems.at[h, d], yr_sems.at[h, d], at(x, up(d), z)
+            )
+            copy.start()
+            y_copies[h, d] = copy
+
+    def along_x(h, k):
+        d = order[k]
+        if d:
+            y_copies[h, d].wait_recv()
+        piece = all_ref.at[x, lax.rem(y + 8 - d, 8), layers[h]]
+        for side in range(2):
+            copy = remote(piece, piece, xs_sems.at[h, side, k], xr_sems.at[h, side, k], beside[side])
+            copy.start()
+            x_copies[h, side, k] = copy
+
+    def onward(h, k):
+        side = k % 2
+        x_copies[h, side, k].wait_recv()
+        piece = all_ref.at[right if side else left, lax.rem(y + 8 - order[k], 8), layers[h]]
+        copy = remote(piece, piece, fs_sems.at[h, k], fr_sems.at[h, k], beside[side])
+        copy.start()
+        forwards[h, k] = copy
+
+    along_y(0, own_ref)
+    keep.wait()
+    for k in range(5):
+        along_x(0, k)
     to_across.wait_recv()
-    other = all_ref.at[x, y, 1 - z]
-    for d in OFFSETS:
-        y_copies[1, d] = remote(other, other, ys_sems.at[1, d], yr_sems.at[1, d], at(x, up(d), z))
-        y_copies[1, d].start()
-    keep.wait()
-    order = (0,) + OFFSETS
-    x_copies = []
-    for k, d in enumerate(order):
-        if d:
-            y_copies[0, d].wait_recv()
-            y_copies[1, d].wait_recv()
-        piece = all_ref.at[x, lax.rem(y + 8 - d, 8)]
-        for side in range(2):
-            copy = remote(piece, piece, xs_sems.at[side, k], xr_sems.at[side, k], beside[side])
-            copy.start()
-            x_copies.append(copy)
-    forwards = []
-    for k, d in enumerate(order):
-        first = k % 2
-        for side in (first, 1 - first):
-            x_copies[2 * k + side].wait_recv()
-            if side == first:
-                source = left if side == 0 else right
-                piece = all_ref.at[source, lax.rem(y + 8 - d, 8)]
-                copy = remote(piece, piece, fs_sems.at[k], fr_sems.at[k], beside[side])
-                copy.start()
-                forwards.append(copy)
-    for copy in forwards:
-        copy.wait_recv()
+    along_y(1, all_ref.at[x, y, 1 - z])
+    along_x(1, 0)
+    for k in range(5, 8):
+        along_x(0, k)
+    onward(0, 0)
+    for k in range(1, 8):
+        along_x(1, k)
+        onward(0, k)
+    for k in range(8):
+        onward(1, k)
+    for h in range(2):
+        for k in range(8):
+            x_copies[h, 1 - k % 2, k].wait_recv()
+            forwards[h, k].wait_recv()
     rows = all_ref.shape[3]
     everyone = all_ref[...].reshape(BAND * rows, all_ref.shape[4])
     partial = jnp.dot(everyone, screening_ref[...], preferred_element_type=F32).astype(BF16)
@@ -155,7 +168,7 @@
     for copy in copies:
         copy.wait_send()
     to_across.wait_send()
-    for copy in [*y_copies.values(), *x_copies, *forwards]:
+    for copy in [*y_copies.values(), *x_copies.values(), *forwards.values()]:
         copy.wait_send()
 
 
@@ -172,45 +185,11 @@
             pltpu.VMEM((PW, PW * rows, width), BF16),
             pltpu.VMEM((PW, PW * rows, width), BF16),
             pltpu.VMEM((PW, rows, width), F32),
-            dma, dma((2,)), dma((2, 8)), dma((2, 8)), dma((2, 8)), dma((2, 8)), dma((8,)), dma((8,)),
+            dma, dma((2,)), dma((2, 8)), dma((2, 8)), dma((2, 2, 8)), dma((2, 2, 8)), dma((2, 8)), dma((2, 8)),
             dma((PW,)), dma((PW,)), dma((PW,)), dma((PW,)),
         ],
         compiler_params=pltpu.CompilerParams(collective_id=0, has_side_effects=True),
     )(own, screening)
-
-
-def exchange_kernel(from_ref, to_ref, own_sem, s_sems, r_sems):
-    band, pw = lax.axis_index("band"), lax.axis_index("pw")
-
-    def over(d):
-        return lax.rem(pw + d, PW)
-
-    barrier = pltpu.get_barrier_semaphore()
-    for d in range(1, PW):
-        pl.semaphore_signal(barrier, inc=1, device_id=(band, over(d)), device_id_type=MESH)
-    own = pltpu.make_async_copy(from_ref.at[pw], to_ref.at[pw], own_sem)
-    own.start()
-    pl.semaphore_wait(barrier, PW - 1)
-    copies = []
-    for d in range(1, PW):
-        copy = remote(from_ref.at[over(d)], to_ref.at[pw], s_sems.at[d], r_sems.at[d], (band, over(d)))
-        copy.start()
-        copies.append(copy)
-    own.wait()
-    for copy in copies:
-        copy.wait()
-
-
-def exchanged(blocks, collective_id):
-    dma = pltpu.SemaphoreType.DMA
-    return pl.pallas_call(
-        exchange_kernel,
-        out_shape=jax.ShapeDtypeStruct(blocks.shape, blocks.dtype),
-        in_specs=[pl.BlockSpec(memory_space=pltpu.VMEM)],
-        out_specs=pl.BlockSpec(memory_space=pltpu.VMEM),
-        scratch_shapes=[dma, dma((PW,)), dma((PW,))],
-        compiler_params=pltpu.CompilerParams(collective_id=collective_id, has_side_effects=True),
-    )(blocks)
 
 
 def body(occupied, virtual, screening, grid_index):
@@ -243,12 +222,13 @@
 
     occ = occupied.reshape(pairs, planes, GRID, GRID).astype(F32)
     density = occ * virtual.reshape(1, planes, GRID, GRID).astype(F32)
-    field = jnp.concatenate(
-        [dot("pxyz,zc->pxyc", density, cos_k), dot("pxyz,zc->pxyc", density, -sin_k)], axis=2
-    )
+    field = dot("pxyz,zc->pxyc", density, jnp.concatenate([cos_k, -sin_k], axis=1))
+    field = jnp.concatenate([field[..., :NK], field[..., NK:]], axis=2)
     field = dot("yk,pxyc->pxkc", to_rows, field).astype(BF16)
     field = field.reshape(pairs, planes, PW, 2 * NJ, NK).transpose(2, 1, 0, 3, 4)
-    pencil = exchanged(field.reshape(PW, planes, pairs * 2 * NJ * NK), 1).reshape(GRID, -1)
+    pencil = lax.all_to_all(
+        field.reshape(PW, planes, pairs * 2 * NJ * NK), "pw", 0, 0, tiled=True
+    ).reshape(GRID, -1)
 
     cos_sin = jnp.concatenate([cos_k, sin_k], axis=1)
     mixed = dot("xm,xk->mk", pencil.astype(F32), cos_sin).reshape(pairs, 2, NJ * NK, 2, NK)
@@ -270,7 +250,7 @@
     real = mixed[0, :, :, 0] - mixed[1, :, :, 1]
     imag = mixed[0, :, :, 1] + mixed[1, :, :, 0]
     pencil = jnp.stack([real, imag], axis=2).astype(BF16).reshape(PW, planes, -1)
-    field = exchanged(pencil, 2).reshape(PW, planes, pairs, 2 * NJ, NK)
+    field = lax.all_to_all(pencil, "pw", 0, 0, tiled=True).reshape(PW, planes, pairs, 2 * NJ, NK)
     field = field.transpose(2, 1, 0, 3, 4).reshape(pairs, planes, PW * 2 * NJ, NK).astype(F32)
     mixed = dot("yk,pxkc->pxyc", to_rows, field)
     norm_out = 1.0 / math.sqrt(NG)

time: 85.9 us -> 83 us (0.966)
  Pallas kernels: 64.7 us -> 41.4 us
  blocking collectives: 0 us -> 10.1 us
  starting transfers between devices: 0 us -> 10.1 us
  waiting for transfers between devices: 0 us -> 3.87 us
  local copies, waits for them, and re-layouts: 9.21 us -> 6.96 us
  matrix products: 8.4 us -> 6.96 us
    pallas_call x2 -> x0, Pallas kernels: 22.3 us -> none  [exchanged(): pl.pallas_call(exchange_kernel, out_shape=jax.ShapeDtypeStruct(blocks.sha...]
    all_to_all x0 -> x1, blocking collectives: none -> 10.1 us  [body(): lax.all_to_all(pencil, 'pw', 0, 0, tiled=True)]
    all_to_all x0 -> x1, starting transfers between devices: none -> 10.1 us  [body(): lax.all_to_all(field.reshape(PW, planes, pairs * 2 * NJ * NK), 'pw', 0, 0...]
    all_to_all x0 -> x1, waiting for transfers between devices: none -> 3.87 us  [body(): lax.all_to_all(field.reshape(PW, planes, pairs * 2 * NJ * NK), 'pw', 0, 0...]
    dot_general x8 -> x7, matrix products: 7.46 us -> 6.02 us  [dot(): return jnp.einsum(spec, a, b, precision=PRECISE, preferred_element_type=F32)]
    pallas_call x1, Pallas kernels: 42.3 us -> 41.4 us  [screened_home(): pl.pallas_call(screen_kernel, out_shape=jax.ShapeDtypeStruct((PW, rows, w...]
    reshape x1, local copies, waits for them, and re-layouts: 1.81 us -> 0.91 us  [body(): lax.all_to_all(pencil, 'pw', 0, 0, tiled=True)]
    dot_general x2, local copies, waits for them, and re-layouts: 1.04 us -> 0.15 us  [dot(): return jnp.einsum(spec, a, b, precision=PRECISE, preferred_element_type=F32)]
  transfers between devices with their start and end apart: 0 -> 1, of which waited for: 0 -> 1; matrix products, arithmetic and copies ran while one was open for 0% -> 2% of each run, Pallas kernels for 0% -> 0%
where the time goes in v5:
time: 83 us; the launch traced here: 82.5 us
  Pallas kernels  41.4 us (50%)
  starting transfers between devices  10.1 us (12%)
  blocking collectives  10.1 us (12%)
  local copies, waits for them, and re-layouts  6.96 us (8%)
  matrix products  6.96 us (8%)
  waiting for transfers between devices  3.87 us (5%)
  other arithmetic  2.89 us (3%)
    pallas_call x1, Pallas kernels, screened_home(): pl.pallas_call(screen_kernel, out_shape=jax.ShapeDtypeStruct((PW, rows, w...  41.4 us
    all_to_all x1, blocking collectives, body(): lax.all_to_all(pencil, 'pw', 0, 0, tiled=True)  10.1 us
    all_to_all x1, starting transfers between devices, body(): lax.all_to_all(field.reshape(PW, planes, pairs * 2 * NJ * NK), 'pw', 0, 0...  10.1 us
    dot_general x7, matrix products, dot(): return jnp.einsum(spec, a, b, precision=PRECISE, preferred_element_type=F32)  6.02 us
    all_to_all x1, waiting for transfers between devices, body(): lax.all_to_all(field.reshape(PW, planes, pairs * 2 * NJ * NK), 'pw', 0, 0...  3.87 us
  transfers between devices with their start and end apart: 1, of which 1 were waited for; matrix products, arithmetic and copies ran while one was open for 2% of the time, Pallas kernels for 0%

profile of v5, /device:TPU:1, one launch (start us, length us, event | category | flops | bytes accessed | tf_op | source)
XLA Modules:
  0.0 82.5 jit_solution(8723554283154378201)
XLA Ops:
  0.0 0.2 fusion.69
  0.2 1.1 %reshape.291 = f32[2,8,64,64]{3,2,1,0:T(8,128)S(1)} reshape(bf16[2,8,4096]{2,1,0:T(8,128)(2,1)} %param.4) | data formatting | bytes 393216 | tf_op jit(solution)/shard_map/convert_element_type | solution.py:223
  1.3 1.0 %reshape.292 = f32[8,64,64]{2,1,0:T(8,128)S(1)} reshape(bf16[1,8,4096]{2,1,0:T(8,128)(2,1)} %param.5) | data formatting | bytes 196608 | tf_op jit(solution)/shard_map/convert_element_type | solution.py:224
  2.3 0.6 fusion.17
  2.9 0.2 fusion.98
  3.1 0.1 broadcast_add_fusion
  3.2 0.2 fusion.66
  3.4 0.1 maximum_maximum_fusion
  3.5 1.8 %fusion.10 = bf16[2,8,80,33]{2,3,1,0:T(8,128)(2,1)S(1)} fusion(f32[2,8,64,33]{3,2,1,0:T(8,128)S(1)} %get-tuple-element.10, f32[2,8,64,33]{3,2,1,0:T(8,128)S(1)} %get-tuple-element.9, f32[128,80,1,1]{0,1,2,3:T(8,128)S(1)} %reshape.294), kind=kOutput, calls=%fused_computation.12 | convolution fusion | flops 64990464 | bytes 395776 | tf_op jit(solution)/shard_map/yk,pxyc->pxkc/dot_general | solution.py:28
  5.3 0.3 copy.69
  5.6 0.1 copy.70
  5.7 1.2 %reshape.285 = bf16[8,8,660]{2,1,0:T(8,128)(2,1)} reshape(bf16[8,8,2,10,33]{4,3,2,1,0:T(8,128)(2,1)S(1)} %copy.70) | data formatting | bytes 168960 | tf_op jit(solution)/shard_map/reshape | solution.py:230
  6.9 10.1 %all-to-all-start = ((bf16[8,8,660]{2,1,0:T(8,128)(2,1)}), bf16[8,8,660]{2,1,0:T(8,128)(2,1)S(1)}, u32[]{:S(2)}, u32[]{:S(2)}) async-start(bf16[8,8,660]{2,1,0:T(8,128)(2,1)} %reshape.285), calls=%async_computation | async-start | bytes 196608 | tf_op jit(solution)/shard_map/all_to_all | solution.py:229
  17.0 0.7 fusion.81
  17.8 0.7 fusion.76
  18.5 3.9 %all-to-all-done = bf16[8,8,660]{2,1,0:T(8,128)(2,1)S(1)} async-done(((bf16[8,8,660]{2,1,0:T(8,128)(2,1)}), bf16[8,8,660]{2,1,0:T(8,128)(2,1)S(1)}, u32[]{:S(2)}, u32[]{:S(2)}) %all-to-all-start) | async-done | bytes 84512 | tf_op jit(solution)/shard_map/all_to_all | solution.py:229
  22.4 0.1 dot_general.38
  22.5 0.3 fusion.30
  22.9 0.5 fusion.5
  23.3 0.6 convert_element_type.117.own_ref
  23.9 41.4 %shard_map.46 = f32[8,4,256]{2,1,0:T(4,128)} custom-call(bf16[4,2048]{1,0:T(4,128)(2,1)} %convert_element_type.117.own_ref, bf16[2048,256]{1,0:T(8,128)(2,1)} %screening_ref.1), custom_call_target="tpu_custom_call" | custom-call | tf_op jit(solution)/shard_map/pallas_call | solution.py:178
  65.4 0.8 convert_element_type.118
  66.1 0.5 fusion.3
  66.6 0.8 convolution_bitcast_fusion
  67.4 0.2 copy.75
  67.7 0.1 copy.77
  67.8 0.1 convert_element_type.119
  67.9 10.1 %all_to_all.10 = bf16[8,8,660]{2,1,0:T(8,128)(2,1)S(1)} all-to-all(bf16[8,8,660]{2,1,0:T(8,128)(2,1)S(1)} %convert_element_type.119), channel_id=1, replica_groups=mesh['band'=64,'pw'=8] {'pw'}, dimensions={0} | all-to-all | bytes 168960 | tf_op jit(solution)/shard_map/all_to_all | solution.py:253
  78.0 0.9 %reshape.288 = bf16[8,8,2,10,33]{4,3,2,1,0:T(8,128)(2,1)S(1)} reshape(bf16[8,8,660]{2,1,0:T(8,128)(2,1)S(1)} %all_to_all.10) | data formatting | bytes 168960 | tf_op jit(solution)/shard_map/reshape | solution.py:253
  79.0 0.1 copy.78
  79.1 0.4 convolution_bitcast_fusion.1
  79.5 1.0 %fusion.20 = f32[2,8,64,64]{3,2,1,0:T(8,128)S(1)} fusion(f32[2,8,128,33]{2,3,1,0:T(8,128)S(1)} %convolution_bitcast_fusion.1, s32[33]{0:T(128)S(1)} %iota_add_fusion.1), kind=kOutput, calls=%fused_computation.22 | convolution fusion | flops 25983936 | bytes 532612 | tf_op jit(solution)/shard_map/pxyc,zc->pxyz/dot_general | solution.py:28
  80.6 1.2 %fusion.9 = f32[8,64,64]{2,1,0:T(8,128)S(1)} fusion(f32[2,8,64,64]{3,2,1,0:T(8,128)S(1)} %reshape.291, f32[2,8,64,64]{3,2,1,0:T(8,128)S(1)} %fusion.20, f32[2,8,128,33]{2,3,1,0:T(8,128)S(1)} %convolution_bitcast_fusion.1, s32[33]{0:T(128)S(1)} %iota_add_fusion.1), kind=kOutput, calls=%fused_computation.8 | convolution fusion | flops 26147776 | bytes 925828 | tf_op jit(solution)/shard_map/pxyc,zc->pxyz/dot_general | solution.py:28
  81.8 0.8 reshape.290
  (11 shorter events, 0.1 us)
Async XLA Ops:
  6.9 15.5 %all-to-all-start = ((bf16[8,8,660]{2,1,0:T(8,128)(2,1)}), bf16[8,8,660]{2,1,0:T(8,128)(2,1)S(1)}, u32[]{:S(2)}, u32[]{:S(2)}) async-start(bf16[8,8,660]{2,1,0:T(8,128)(2,1)} %reshape.285), calls=%async_computation | async-start | bytes 196608 | tf_op jit(solution)/shard_map/all_to_all | solution.py:229

commit v6 on v5

--- a/solution.py
+++ b/solution.py
@@ -121,20 +121,35 @@
         onward(0, k)
     for k in range(8):
         onward(1, k)
-    for h in range(2):
-        for k in range(8):
-            x_copies[h, 1 - k % 2, k].wait_recv()
-            forwards[h, k].wait_recv()
     rows = all_ref.shape[3]
-    everyone = all_ref[...].reshape(BAND * rows, all_ref.shape[4])
-    partial = jnp.dot(everyone, screening_ref[...], preferred_element_type=F32).astype(BF16)
-    part_ref[...] = partial.reshape(part_ref.shape)
-
-    copies = []
-    for d in range(1, PW):
-        copy = remote(part_ref.at[over(d)], landed.at[pw], ps_sems.at[d], pr_sems.at[d], (band, over(d)))
-        copy.start()
-        copies.append(copy)
+
+    def part_send(q):
+        d = lax.rem(q - pw + PW, PW)
+        return remote(part_ref.at[q], landed.at[pw], ps_sems.at[d], pr_sems.at[d], (band, q))
+
+    def screen(x_at):
+        block = all_ref[x_at].reshape(16 * rows, all_ref.shape[4])
+        product = jnp.dot(block, screening_ref[...], preferred_element_type=F32).astype(BF16)
+        part_ref[pl.ds(2 * x_at, 2)] = product.reshape(2, PW * rows, product.shape[1])
+        for e in range(2):
+            q = 2 * x_at + e
+
+            @pl.when(q != pw)
+            def _():
+                part_send(q).start()
+
+    screen(x)
+    for side in (1, 0):
+        for h in range(2):
+            for k in range(8):
+                if k % 2 != side:
+                    x_copies[h, side, k].wait_recv()
+        screen(right if side else left)
+    for copy in forwards.values():
+        copy.wait_recv()
+    screen(lax.rem(x + 2, 4))
+
+    copies = [part_send(over(d)) for d in range(1, PW)]
     total = part_ref[pw].astype(F32)
     for d in range(1, PW):
         copies[d - 1].wait_recv()

time: 83 us -> 83.1 us (level)
  blocking collectives: 10.1 us -> 12.6 us
  Pallas kernels: 41.4 us -> 39 us
    all_to_all x1, blocking collectives: 10.1 us -> 12.6 us  [body(): lax.all_to_all(pencil, 'pw', 0, 0, tiled=True)]
    pallas_call x1, Pallas kernels: 41.4 us -> 39 us  [screened_home(): pl.pallas_call(screen_kernel, out_shape=jax.ShapeDtypeStruct((PW, rows, w...]
where the time goes in v6:
time: 83.1 us; the launch traced here: 82.6 us
  Pallas kernels  39 us (47%)
  blocking collectives  12.6 us (15%)
  starting transfers between devices  10.1 us (12%)
  local copies, waits for them, and re-layouts  6.96 us (8%)
  matrix products  6.96 us (8%)
  waiting for transfers between devices  3.87 us (5%)
  other arithmetic  2.89 us (3%)
    pallas_call x1, Pallas kernels, screened_home(): pl.pallas_call(screen_kernel, out_shape=jax.ShapeDtypeStruct((PW, rows, w...  39 us
    all_to_all x1, blocking collectives, body(): lax.all_to_all(pencil, 'pw', 0, 0, tiled=True)  12.6 us
    all_to_all x1, starting transfers between devices, body(): lax.all_to_all(field.reshape(PW, planes, pairs * 2 * NJ * NK), 'pw', 0, 0...  10.1 us
    dot_general x7, matrix products, dot(): return jnp.einsum(spec, a, b, precision=PRECISE, preferred_element_type=F32)  6.02 us
    all_to_all x1, waiting for transfers between devices, body(): lax.all_to_all(field.reshape(PW, planes, pairs * 2 * NJ * NK), 'pw', 0, 0...  3.87 us
  transfers between devices with their start and end apart: 1, of which 1 were waited for; matrix products, arithmetic and copies ran while one was open for 2% of the time, Pallas kernels for 0%

profile of v6, /device:TPU:1, one launch (start us, length us, event | category | flops | bytes accessed | tf_op | source)
XLA Modules:
  0.0 82.6 jit_solution(13750712982446535816)
XLA Ops:
  0.0 0.2 fusion.69
  0.2 1.1 %reshape.291 = f32[2,8,64,64]{3,2,1,0:T(8,128)S(1)} reshape(bf16[2,8,4096]{2,1,0:T(8,128)(2,1)} %param.4) | data formatting | bytes 393216 | tf_op jit(solution)/shard_map/convert_element_type | solution.py:238
  1.3 1.0 %reshape.292 = f32[8,64,64]{2,1,0:T(8,128)S(1)} reshape(bf16[1,8,4096]{2,1,0:T(8,128)(2,1)} %param.5) | data formatting | bytes 196608 | tf_op jit(solution)/shard_map/convert_element_type | solution.py:239
  2.3 0.6 fusion.17
  2.9 0.2 fusion.98
  3.1 0.1 broadcast_add_fusion
  3.2 0.2 fusion.66
  3.4 0.1 maximum_maximum_fusion
  3.5 1.8 %fusion.10 = bf16[2,8,80,33]{2,3,1,0:T(8,128)(2,1)S(1)} fusion(f32[2,8,64,33]{3,2,1,0:T(8,128)S(1)} %get-tuple-element.10, f32[2,8,64,33]{3,2,1,0:T(8,128)S(1)} %get-tuple-element.9, f32[128,80,1,1]{0,1,2,3:T(8,128)S(1)} %reshape.294), kind=kOutput, calls=%fused_computation.12 | convolution fusion | flops 64990464 | bytes 395776 | tf_op jit(solution)/shard_map/yk,pxyc->pxkc/dot_general | solution.py:28
  5.3 0.3 copy.69
  5.6 0.1 copy.70
  5.7 1.2 %reshape.285 = bf16[8,8,660]{2,1,0:T(8,128)(2,1)} reshape(bf16[8,8,2,10,33]{4,3,2,1,0:T(8,128)(2,1)S(1)} %copy.70) | data formatting | bytes 168960 | tf_op jit(solution)/shard_map/reshape | solution.py:245
  6.9 10.1 %all-to-all-start = ((bf16[8,8,660]{2,1,0:T(8,128)(2,1)}), bf16[8,8,660]{2,1,0:T(8,128)(2,1)S(1)}, u32[]{:S(2)}, u32[]{:S(2)}) async-start(bf16[8,8,660]{2,1,0:T(8,128)(2,1)} %reshape.285), calls=%async_computation | async-start | bytes 196608 | tf_op jit(solution)/shard_map/all_to_all | solution.py:244
  17.0 0.7 fusion.81
  17.8 0.7 fusion.76
  18.5 3.9 %all-to-all-done = bf16[8,8,660]{2,1,0:T(8,128)(2,1)S(1)} async-done(((bf16[8,8,660]{2,1,0:T(8,128)(2,1)}), bf16[8,8,660]{2,1,0:T(8,128)(2,1)S(1)}, u32[]{:S(2)}, u32[]{:S(2)}) %all-to-all-start) | async-done | bytes 84512 | tf_op jit(solution)/shard_map/all_to_all | solution.py:244
  22.4 0.1 dot_general.38
  22.5 0.3 fusion.30
  22.9 0.5 fusion.5
  23.3 0.6 convert_element_type.117.own_ref
  23.9 39.0 %shard_map.46 = f32[8,4,256]{2,1,0:T(4,128)} custom-call(bf16[4,2048]{1,0:T(4,128)(2,1)} %convert_element_type.117.own_ref, bf16[2048,256]{1,0:T(8,128)(2,1)} %screening_ref.1), custom_call_target="tpu_custom_call" | custom-call | tf_op jit(solution)/shard_map/pallas_call | solution.py:193
  62.9 0.8 convert_element_type.118
  63.7 0.5 fusion.3
  64.2 0.8 convolution_bitcast_fusion
  65.0 0.2 copy.75
  65.2 0.1 copy.77
  65.4 0.1 convert_element_type.119
  65.5 12.6 %all_to_all.10 = bf16[8,8,660]{2,1,0:T(8,128)(2,1)S(1)} all-to-all(bf16[8,8,660]{2,1,0:T(8,128)(2,1)S(1)} %convert_element_type.119), channel_id=1, replica_groups=mesh['band'=64,'pw'=8] {'pw'}, dimensions={0} | all-to-all | bytes 168960 | tf_op jit(solution)/shard_map/all_to_all | solution.py:268
  78.1 0.9 %reshape.288 = bf16[8,8,2,10,33]{4,3,2,1,0:T(8,128)(2,1)S(1)} reshape(bf16[8,8,660]{2,1,0:T(8,128)(2,1)S(1)} %all_to_all.10) | data formatting | bytes 168960 | tf_op jit(solution)/shard_map/reshape | solution.py:268
  79.0 0.1 copy.78
  79.1 0.4 convolution_bitcast_fusion.1
  79.6 1.0 %fusion.20 = f32[2,8,64,64]{3,2,1,0:T(8,128)S(1)} fusion(f32[2,8,128,33]{2,3,1,0:T(8,128)S(1)} %convolution_bitcast_fusion.1, s32[33]{0:T(128)S(1)} %iota_add_fusion.1), kind=kOutput, calls=%fused_computation.22 | convolution fusion | flops 25983936 | bytes 532612 | tf_op jit(solution)/shard_map/pxyc,zc->pxyz/dot_general | solution.py:28
  80.6 1.2 %fusion.9 = f32[8,64,64]{2,1,0:T(8,128)S(1)} fusion(f32[2,8,64,64]{3,2,1,0:T(8,128)S(1)} %reshape.291, f32[2,8,64,64]{3,2,1,0:T(8,128)S(1)} %fusion.20, f32[2,8,128,33]{2,3,1,0:T(8,128)S(1)} %convolution_bitcast_fusion.1, s32[33]{0:T(128)S(1)} %iota_add_fusion.1), kind=kOutput, calls=%fused_computation.8 | convolution fusion | flops 26147776 | bytes 925828 | tf_op jit(solution)/shard_map/pxyc,zc->pxyz/dot_general | solution.py:28
  81.8 0.8 reshape.290
  (11 shorter events, 0.1 us)
Async XLA Ops:
  6.9 15.5 %all-to-all-start = ((bf16[8,8,660]{2,1,0:T(8,128)(2,1)}), bf16[8,8,660]{2,1,0:T(8,128)(2,1)S(1)}, u32[]{:S(2)}, u32[]{:S(2)}) async-start(bf16[8,8,660]{2,1,0:T(8,128)(2,1)} %reshape.285), calls=%async_computation | async-start | bytes 196608 | tf_op jit(solution)/shard_map/all_to_all | solution.py:244

commit v7 on v6

--- a/solution.py
+++ b/solution.py
@@ -14,7 +14,7 @@
 PW = 8
 BAND = 64
 NJ = 5
-PRECISE = lax.Precision.HIGHEST
+PRECISE = lax.Precision.HIGH
 F32 = jnp.float32
 BF16 = jnp.bfloat16
 

time: 83.1 us -> 80.9 us (0.974)
  matrix products: 6.96 us -> 4.79 us
    dot_general x7, matrix products: 6.02 us -> 3.84 us  [dot(): return jnp.einsum(spec, a, b, precision=PRECISE, preferred_element_type=F32)]
where the time goes in v7:
time: 80.9 us; the launch traced here: 80.4 us
  Pallas kernels  39 us (48%)
  blocking collectives  12.5 us (15%)
  starting transfers between devices  10.1 us (12%)
  local copies, waits for them, and re-layouts  6.96 us (9%)
  matrix products  4.79 us (6%)
  waiting for transfers between devices  3.87 us (5%)
  other arithmetic  2.89 us (4%)
    pallas_call x1, Pallas kernels, screened_home(): pl.pallas_call(screen_kernel, out_shape=jax.ShapeDtypeStruct((PW, rows, w...  39 us
    all_to_all x1, blocking collectives, body(): lax.all_to_all(pencil, 'pw', 0, 0, tiled=True)  12.5 us
    all_to_all x1, starting transfers between devices, body(): lax.all_to_all(field.reshape(PW, planes, pairs * 2 * NJ * NK), 'pw', 0, 0...  10.1 us
    all_to_all x1, waiting for transfers between devices, body(): lax.all_to_all(field.reshape(PW, planes, pairs * 2 * NJ * NK), 'pw', 0, 0...  3.87 us
    dot_general x7, matrix products, dot(): return jnp.einsum(spec, a, b, precision=PRECISE, preferred_element_type=F32)  3.84 us
  transfers between devices with their start and end apart: 1, of which 1 were waited for; matrix products, arithmetic and copies ran while one was open for 2% of the time, Pallas kernels for 0%

profile of v7, /device:TPU:1, one launch (start us, length us, event | category | flops | bytes accessed | tf_op | source)
XLA Modules:
  0.0 80.4 jit_solution(5987704422959756666)
XLA Ops:
  0.0 0.2 fusion.69
  0.2 1.1 %reshape.291 = f32[2,8,64,64]{3,2,1,0:T(8,128)S(1)} reshape(bf16[2,8,4096]{2,1,0:T(8,128)(2,1)} %param.4) | data formatting | bytes 393216 | tf_op jit(solution)/shard_map/convert_element_type | solution.py:238
  1.3 1.0 %reshape.292 = f32[8,64,64]{2,1,0:T(8,128)S(1)} reshape(bf16[1,8,4096]{2,1,0:T(8,128)(2,1)} %param.5) | data formatting | bytes 196608 | tf_op jit(solution)/shard_map/convert_element_type | solution.py:239
  2.3 0.4 fusion.17
  2.7 0.2 fusion.98
  2.9 0.1 broadcast_add_fusion
  3.0 0.2 fusion.66
  3.2 0.1 maximum_maximum_fusion
  3.3 1.0 %fusion.10 = bf16[2,8,80,33]{2,3,1,0:T(8,128)(2,1)S(1)} fusion(f32[2,8,64,33]{3,2,1,0:T(8,128)S(1)} %get-tuple-element.10, f32[2,8,64,33]{3,2,1,0:T(8,128)S(1)} %get-tuple-element.9, f32[128,80,1,1]{0,1,2,3:T(8,128)S(1)} %reshape.294), kind=kOutput, calls=%fused_computation.12 | convolution fusion | flops 32550144 | bytes 395776 | tf_op jit(solution)/shard_map/yk,pxyc->pxkc/dot_general | solution.py:28
  4.3 0.3 copy.69
  4.6 0.1 copy.70
  4.7 1.2 %reshape.285 = bf16[8,8,660]{2,1,0:T(8,128)(2,1)} reshape(bf16[8,8,2,10,33]{4,3,2,1,0:T(8,128)(2,1)S(1)} %copy.70) | data formatting | bytes 168960 | tf_op jit(solution)/shard_map/reshape | solution.py:245
  5.9 10.1 %all-to-all-start = ((bf16[8,8,660]{2,1,0:T(8,128)(2,1)}), bf16[8,8,660]{2,1,0:T(8,128)(2,1)S(1)}, u32[]{:S(2)}, u32[]{:S(2)}) async-start(bf16[8,8,660]{2,1,0:T(8,128)(2,1)} %reshape.285), calls=%async_computation | async-start | bytes 196608 | tf_op jit(solution)/shard_map/all_to_all | solution.py:244
  16.0 0.7 fusion.81
  16.8 0.7 fusion.76
  17.5 3.9 %all-to-all-done = bf16[8,8,660]{2,1,0:T(8,128)(2,1)S(1)} async-done(((bf16[8,8,660]{2,1,0:T(8,128)(2,1)}), bf16[8,8,660]{2,1,0:T(8,128)(2,1)S(1)}, u32[]{:S(2)}, u32[]{:S(2)}) %all-to-all-start) | async-done | bytes 84512 | tf_op jit(solution)/shard_map/all_to_all | solution.py:244
  21.4 0.1 dot_general.38
  21.5 0.2 fusion.30
  21.8 0.5 fusion.5
  22.3 0.6 convert_element_type.117.own_ref
  22.9 39.0 %shard_map.46 = f32[8,4,256]{2,1,0:T(4,128)} custom-call(bf16[4,2048]{1,0:T(4,128)(2,1)} %convert_element_type.117.own_ref, bf16[2048,256]{1,0:T(8,128)(2,1)} %screening_ref.1), custom_call_target="tpu_custom_call" | custom-call | tf_op jit(solution)/shard_map/pallas_call | solution.py:193
  61.9 0.8 convert_element_type.118
  62.7 0.5 fusion.3
  63.2 0.5 convolution_bitcast_fusion
  63.6 0.2 copy.75
  63.9 0.1 copy.77
  64.1 0.1 convert_element_type.119
  64.2 12.5 %all_to_all.10 = bf16[8,8,660]{2,1,0:T(8,128)(2,1)S(1)} all-to-all(bf16[8,8,660]{2,1,0:T(8,128)(2,1)S(1)} %convert_element_type.119), channel_id=1, replica_groups=mesh['band'=64,'pw'=8] {'pw'}, dimensions={0} | all-to-all | bytes 168960 | tf_op jit(solution)/shard_map/all_to_all | solution.py:268
  76.7 0.9 %reshape.288 = bf16[8,8,2,10,33]{4,3,2,1,0:T(8,128)(2,1)S(1)} reshape(bf16[8,8,660]{2,1,0:T(8,128)(2,1)S(1)} %all_to_all.10) | data formatting | bytes 168960 | tf_op jit(solution)/shard_map/reshape | solution.py:268
  77.7 0.1 copy.78
  77.8 0.3 convolution_bitcast_fusion.1
  78.2 0.7 fusion.20
  78.8 0.8 fusion.9
  79.6 0.8 reshape.290
  (11 shorter events, 0.1 us)
Async XLA Ops:
  5.9 15.5 %all-to-all-start = ((bf16[8,8,660]{2,1,0:T(8,128)(2,1)}), bf16[8,8,660]{2,1,0:T(8,128)(2,1)S(1)}, u32[]{:S(2)}, u32[]{:S(2)}) async-start(bf16[8,8,660]{2,1,0:T(8,128)(2,1)} %reshape.285), calls=%async_computation | async-start | bytes 196608 | tf_op jit(solution)/shard_map/all_to_all | solution.py:244
